TPU v7x, 32 devices: a whole 2x2x4 slice. The times are simulated.
32 devices in a mesh: row: 4 (over z), col: 8 (over y, x, core).
Axes of the slice: x: 2, y: 2, z: 4, core: 2. Of those that a mesh axis runs over, the one named last changes fastest.
Arguments:
- object_field: bfloat16 [2, 2048, 4096], P(None, 'row', 'col'), may hold values from -6 to 6
- probe_modes: float32 [2, 2, 256, 256], replicated, may hold values from -6 to 6
- measured_amp: bfloat16 [4, 8, 8, 256, 256], P('row', 'col'), may hold values from 0.25 to 8
- scan_positions: int32 [4, 8, 2, 8], P('row', 'col'), may hold values from 0 to 512
- frame_counts: int32 [4, 8], P('row', 'col'), may hold values from 1 to 8, as said below
Outputs:
- object_grad: float32 [2, 2048, 4096], P(None, 'row', 'col')
- probe_grad: float32 [2, 2, 256, 256], replicated
Inputs may be any that keep to these rules, and one draw needn't show every extreme that they name: `frame_counts`: live frames of a tile; slots at or past it are ignored; some tile has exactly 8.
All inputs are finite; a program needn't handle non-finite values.
Results may differ from a plain program's by a relative error of at most 0.0059.
The roundings to bfloat16 on the way count: a program that leaves them out, or rounds other values in their place, can miss the bound.
Values may be sent and summed in bfloat16 or wider, within the bound.
A program may use at most 64 MiB of HBM per device.

v0:
```python
import functools
import math

import jax
import jax.numpy as jnp
import numpy as np
from jax import lax
from jax.experimental import pallas as pl
from jax.experimental.pallas import tpu as pltpu
from jax.sharding import PartitionSpec as P

HALO = 128
LANES = 128


MESH = pl.DeviceIdType.MESH
SIDES = [(dr, dc) for dr in (-1, 0, 1) for dc in (-1, 0, 1) if (dr, dc) != (0, 0)]


def position():
    return (
        lax.axis_index("row"),
        lax.axis_index("col"),
        lax.axis_size("row"),
        lax.axis_size("col"),
    )


def exists(side):
    row, col, rows, cols = position()
    dr, dc = side
    inside = jnp.bool_(True)
    if dr:
        inside = row + dr >= 0 if dr < 0 else row + dr < rows
    if dc:
        other = col + dc >= 0 if dc < 0 else col + dc < cols
        inside = jnp.logical_and(inside, other) if dr else other
    return inside


def at_side(side):
    row, col, _, _ = position()
    return (row + side[0], col + side[1])


def opposite(side):
    return (-side[0], -side[1])


def part(step, margin, inner):
    return {-1: slice(0, margin), 0: slice(margin, margin + inner), 1: slice(margin + inner, None)}[
        step
    ]


def edge(step, margin, inner):
    return {-1: slice(0, margin), 0: slice(0, inner), 1: slice(inner - margin, inner)}[step]


def to_side(side, index, source, landing, send_sems, recv_sems):
    return pltpu.make_async_remote_copy(
        src_ref=source,
        dst_ref=landing,
        send_sem=send_sems.at[index],
        recv_sem=recv_sems.at[index],
        device_id=at_side(side),
        device_id_type=MESH,
    )


def halo_kernel(whole_ref, ext_ref, *scratch):
    landings, (send_sems, recv_sems) = scratch[: len(SIDES)], scratch[len(SIDES) : -2]
    object_ref, load_sem = scratch[-2:]
    load = pltpu.make_async_copy(whole_ref, object_ref, load_sem)
    load.start()
    side_rows, side_cols = object_ref.shape[1:]
    barrier = pltpu.get_barrier_semaphore()
    count = jnp.int32(0)
    for side in SIDES:

        @pl.when(exists(side))
        def _(side=side):
            pl.semaphore_signal(barrier, inc=1, device_id=at_side(side), device_id_type=MESH)

        count = count + exists(side).astype(jnp.int32)
    pl.semaphore_wait(barrier, count)
    load.wait()

    def copy(index):
        dr, dc = SIDES[index]
        source = object_ref.at[:, edge(dr, HALO, side_rows), edge(dc, HALO, side_cols)]
        return to_side(SIDES[index], index, source, landings[index], send_sems, recv_sems)

    for index, side in enumerate(SIDES):

        @pl.when(exists(side))
        def _(index=index):
            copy(index).start()

    for t in range(side_cols // LANES):
        ext_ref[:, HALO // LANES + t, HALO : HALO + side_rows, :] = object_ref[
            :, :, t * LANES : (t + 1) * LANES
        ].astype(jnp.float32)
    spare = ext_ref.shape[1] - 1
    ext_ref[:, spare] = jnp.zeros((2, ext_ref.shape[2], LANES), jnp.float32)
    for index, side in enumerate(SIDES):
        dr, dc = opposite(side)
        rows = part(dr, HALO, side_rows)
        tiles = range(spare)[part(dc, HALO // LANES, side_cols // LANES)]

        @pl.when(exists((dr, dc)))
        def _(index=index, rows=rows, tiles=tiles):
            copy(index).wait_recv()
            for k, t in enumerate(tiles):
                ext_ref[:, t, rows, :] = landings[index][
                    :, :, k * LANES : (k + 1) * LANES
                ].astype(jnp.float32)

        @pl.when(jnp.logical_not(exists((dr, dc))))
        def _(rows=rows, tiles=tiles, index=index):
            for t in tiles:
                ext_ref[:, t, rows, :] = jnp.zeros(
                    (2, landings[index].shape[1], LANES), ext_ref.dtype
                )

    for index, side in enumerate(SIDES):

        @pl.when(exists(side))
        def _(index=index):
            copy(index).wait_send()


def halo_call(object_field):
    _, side_rows, side_cols = object_field.shape
    vmem = pl.BlockSpec(memory_space=pltpu.VMEM)
    landings = []
    for dr, dc in SIDES:
        landings.append(
            pltpu.VMEM((2, HALO if dr else side_rows, HALO if dc else side_cols), object_field.dtype)
        )
    sems = pltpu.SemaphoreType.DMA((len(SIDES),))
    return pl.pallas_call(
        halo_kernel,
        out_shape=jax.ShapeDtypeStruct(
            (2, (side_cols + 2 * HALO) // LANES + 1, side_rows + 2 * HALO, LANES), jnp.float32
        ),
        in_specs=[pl.BlockSpec(memory_space=pltpu.HBM)],
        out_specs=vmem,
        scratch_shapes=landings
        + [sems, sems, pltpu.VMEM(object_field.shape, object_field.dtype), pltpu.SemaphoreType.DMA],
        compiler_params=pltpu.CompilerParams(
            collective_id=0, has_side_effects=True, vmem_limit_bytes=14 * 1024 * 1024
        ),
        name="halo",
    )(object_field)


def reduce_kernel(scale, acc_ref, pacc_ref, grad_ref, probe_ref, *scratch):
    count = len(SIDES)
    sends, landings, rest = scratch[:count], scratch[count : 2 * count], scratch[2 * count :]
    psend, pair_recv, merged, precv, zsend, zrecv, full = rest[:7]
    side_sems, pair_sems, col_sems, row_sems = rest[7:]
    row, col, n_row, n_col = position()
    side_rows, side_cols = grad_ref.shape[1:]
    margin = HALO // LANES
    inner = side_cols // LANES
    for index, (dr, dc) in enumerate(SIDES):
        tiles = range(inner + 2 * margin)[part(dc, margin, inner)]
        rows = part(dr, HALO, side_rows)
        for k, t in enumerate(tiles):
            sends[index][:, k] = acc_ref[:, t, rows, :].astype(jnp.bfloat16)
    psend[...] = pacc_ref[...].astype(jnp.bfloat16)

    barrier = pltpu.get_barrier_semaphore()
    waits = jnp.int32(n_row + n_col - 2)
    for k in range(1, n_col):
        pl.semaphore_signal(
            barrier, inc=1, device_id=(row, lax.rem(col + k, n_col)), device_id_type=MESH
        )
    for k in range(1, n_row):
        pl.semaphore_signal(
            barrier, inc=1, device_id=(lax.rem(row + k, n_row), col), device_id_type=MESH
        )
    for side in SIDES:
        if side[0] and side[1]:

            @pl.when(exists(side))
            def _(side=side):
                pl.semaphore_signal(barrier, inc=1, device_id=at_side(side), device_id_type=MESH)

            waits = waits + exists(side).astype(jnp.int32)
    pl.semaphore_wait(barrier, waits)

    share = psend.shape[0] // n_col
    piece = share // n_row
    chip, core = col // 2, lax.rem(col, 2)
    n_chip = n_col // 2
    sibling = (row, 2 * chip + 1 - core)

    def to_peer(source, landing, sems, which, k, device):
        return pltpu.make_async_remote_copy(
            src_ref=source,
            dst_ref=landing,
            send_sem=sems.at[which, k - 1],
            recv_sem=sems.at[which + 1, k - 1],
            device_id=device,
            device_id_type=MESH,
        )

    def chip_at(k):
        return lax.rem(chip + k, n_chip)

    def chip_from(k):
        return lax.rem(chip + n_chip - k, n_chip)

    def chip_peer(k):
        return (row, 2 * chip_at(k) + core)

    def row_peer(k):
        return (lax.rem(row + k, n_row), col)

    def share_of(ref, index):
        return ref.at[pl.ds(pl.multiple_of(index * share, share), share)]

    def pair_copy(k):
        source = share_of(psend, 2 * chip_at(k) + 1 - core)
        return to_peer(source, pair_recv.at[k], pair_sems, 0, k + 1, sibling)

    def scatter_copy(k):
        return to_peer(merged.at[k - 1], precv.at[k - 1], col_sems, 0, k, chip_peer(k))

    def row_scatter_copy(k):
        target = lax.rem(row + k, n_row)
        return to_peer(
            zsend.at[pl.ds(pl.multiple_of(target * piece, piece), piece)],
            zrecv.at[k - 1],
            row_sems,
            0,
            k,
            row_peer(k),
        )

    def piece_of(index):
        start = pl.multiple_of(col * share + index * piece, piece)
        return full.at[pl.ds(start, piece)]

    def row_gather_copy(k, owner):
        return to_peer(piece_of(row), piece_of(owner), row_sems, 2, k, row_peer(k))

    def gather_copy(k, owner):
        return to_peer(share_of(full, col), share_of(full, owner), col_sems, 2, k, chip_peer(k))

    def forward_copy(k, side):
        source = share_of(full, 2 * chip_from(k) + core)
        landing = share_of(full, 2 * chip_from(k) + side)
        return to_peer(source, landing, pair_sems, 2, k + 1, sibling)

    def side_copy(index):
        return to_side(
            SIDES[index], index, sends[index], landings[index], side_sems.at[0], side_sems.at[1]
        )

    order = list(range(1, n_chip)) + [0]
    for k in order:
        pair_copy(k).start()

    def start_sides(chosen):
        for index, side in enumerate(SIDES):
            if chosen(side):

                @pl.when(exists(side))
                def _(index=index):
                    side_copy(index).start()

    start_sides(lambda side: side[1] == 0)
    def merge(k):
        pair_copy(k).wait_recv()
        index = 2 * chip_at(k) + core
        own = pacc_ref[pl.ds(pl.multiple_of(index * share, share), share), :]
        return own + pair_recv[k].astype(jnp.float32)

    for k in range(1, n_chip):
        merged[k - 1] = merge(k).astype(jnp.bfloat16)
        scatter_copy(k).start()
    total = merge(0)
    for t in range(inner):
        grad_ref[:, :, t * LANES : (t + 1) * LANES] = acc_ref[
            :, margin + t, HALO : HALO + side_rows, :
        ]
    for k in range(1, n_chip):
        scatter_copy(k).wait_recv()
        total = total + precv[k - 1].astype(jnp.float32)
    zsend[...] = total
    for k in range(1, n_row):
        row_scatter_copy(k).start()
    start_sides(lambda side: side[0] == 0)
    start_sides(lambda side: side[0] != 0 and side[1] != 0)
    own = zsend[pl.ds(pl.multiple_of(row * piece, piece), piece), :]
    for k in range(1, n_row):
        row_scatter_copy(k).wait_recv()
        own = own + zrecv[k - 1]
    start = pl.multiple_of(col * share + row * piece, piece)
    full[pl.ds(start, piece), :] = (own * scale).astype(jnp.bfloat16)
    for k in range(1, n_row):
        row_gather_copy(k, row).start()
    for k in range(1, n_row):
        row_gather_copy(k, lax.rem(row + n_row - k, n_row)).wait_recv()
    for k in range(1, n_chip):
        gather_copy(k, col).start()
    forward_copy(0, core).start()
    for k in range(1, n_chip):
        gather_copy(k, 2 * chip_from(k) + core).wait_recv()
        forward_copy(k, core).start()

    for index, side in enumerate(SIDES):
        dr, dc = opposite(side)
        rows = edge(dr, HALO, side_rows)
        tiles = range(inner)[edge(dc, margin, inner)]

        @pl.when(exists((dr, dc)))
        def _(index=index, rows=rows, tiles=tiles):
            side_copy(index).wait_recv()
            for k, t in enumerate(tiles):
                grad_ref[:, rows, t * LANES : (t + 1) * LANES] += landings[index][:, k].astype(
                    jnp.float32
                )

    for k in range(n_chip):
        forward_copy(k, 1 - core).wait_recv()
    parts, modes, fs, width = probe_ref.shape
    at = 0
    for p in range(parts):
        for m in range(modes):
            for t in range(width // LANES):
                probe_ref[p, m, :, t * LANES : (t + 1) * LANES] = full[at : at + fs, :].astype(
                    jnp.float32
                )
                at += fs
    for k in range(1, n_chip):
        scatter_copy(k).wait_send()
        gather_copy(k, col).wait_send()
    for k in range(n_chip):
        pair_copy(k).wait_send()
        forward_copy(k, core).wait_send()
    for k in range(1, n_row):
        row_scatter_copy(k).wait_send()
        row_gather_copy(k, row).wait_send()
    for index, side in enumerate(SIDES):

        @pl.when(exists(side))
        def _(index=index):
            side_copy(index).wait_send()


def reduce_call(acc, probe_flat, object_shape, probe_shape, scale):
    n_row, n_col = lax.axis_size("row"), lax.axis_size("col")
    _, side_rows, side_cols = object_shape
    inner = side_cols // LANES
    margin = HALO // LANES
    vmem = pl.BlockSpec(memory_space=pltpu.VMEM)
    buffers = []
    for dr, dc in SIDES:
        buffers.append(
            pltpu.VMEM(
                (2, margin if dc else inner, HALO if dr else side_rows, LANES), jnp.bfloat16
            )
        )
    total_rows = probe_flat.shape[0]
    share = total_rows // n_col
    piece = share // n_row
    n_chip = n_col // 2
    return pl.pallas_call(
        functools.partial(reduce_kernel, scale),
        out_shape=(
            jax.ShapeDtypeStruct(object_shape, jnp.float32),
            jax.ShapeDtypeStruct(probe_shape, jnp.float32),
        ),
        in_specs=[vmem, vmem],
        out_specs=(vmem, vmem),
        scratch_shapes=buffers
        + buffers
        + [
            pltpu.VMEM((total_rows, LANES), jnp.bfloat16),
            pltpu.VMEM((n_chip, share, LANES), jnp.bfloat16),
            pltpu.VMEM((n_chip - 1, share, LANES), jnp.bfloat16),
            pltpu.VMEM((n_chip - 1, share, LANES), jnp.bfloat16),
            pltpu.VMEM((share, LANES), jnp.float32),
            pltpu.VMEM((n_row - 1, piece, LANES), jnp.float32),
            pltpu.VMEM((total_rows, LANES), jnp.bfloat16),
            pltpu.SemaphoreType.DMA((2, len(SIDES))),
            pltpu.SemaphoreType.DMA((4, n_chip)),
            pltpu.SemaphoreType.DMA((4, n_chip - 1)),
            pltpu.SemaphoreType.DMA((4, n_row - 1)),
        ],
        compiler_params=pltpu.CompilerParams(
            collective_id=1, has_side_effects=True, vmem_limit_bytes=20 * 1024 * 1024
        ),
        name="reduce",
    )(acc, probe_flat)


def fourier_tables(frame_side):
    indices = np.arange(frame_side)
    product = indices[:, None] * indices[None, :] % frame_side
    angles = 2.0 * math.pi / frame_side * product
    norm_scale = 1.0 / math.sqrt(frame_side)
    return (
        jnp.asarray((np.cos(angles) * norm_scale).astype(np.float32)).astype(jnp.bfloat16),
        jnp.asarray((-np.sin(angles) * norm_scale).astype(np.float32)).astype(jnp.bfloat16),
    )


CHUNK = 32


def dot32(left, right):
    return jnp.dot(left, right, preferred_element_type=jnp.float32)


def frames_kernel(
    count_ref, at_ref, ext_ref, probe_ref, amp_ref, tr_ref, ti_ref, acc_ref, pacc_ref,
    fwd, inv, *buffers,
):
    fs = probe_ref.shape[-1]
    modes = probe_ref.shape[1]
    lane_tiles = fs // LANES
    last_slot = amp_ref.shape[0] - 1
    live = count_ref[0]
    even, odd = buffers[:4], buffers[4:]
    acc_ref[...] = jnp.zeros(acc_ref.shape, jnp.float32)
    pacc_ref[...] = jnp.zeros(pacc_ref.shape, jnp.float32)
    odd[2][...] = jnp.zeros(odd[2].shape, jnp.float32)
    odd[3][...] = jnp.zeros(odd[3].shape, jnp.float32)
    table_real, table_imag = tr_ref[...], ti_ref[...]
    minus = -table_imag
    fwd[:fs, :fs] = table_real
    fwd[:fs, fs:] = minus
    fwd[fs:, :fs] = table_imag
    fwd[fs:, fs:] = table_real
    inv[:fs, :fs] = table_real
    inv[:fs, fs:] = table_imag
    inv[fs:, :fs] = minus
    inv[fs:, fs:] = table_real

    def two_sided(buffer, left_table, right_table):
        stage, half, wide, _ = buffer
        for m in range(modes):
            both = dot32(left_table[...], stage[:, m * fs : (m + 1) * fs])
            half[m * fs : (m + 1) * fs, :fs] = both[:fs].astype(jnp.bfloat16)
            half[m * fs : (m + 1) * fs, fs:] = both[fs:].astype(jnp.bfloat16)
        wide[...] = dot32(half[...], right_table[...])

    def make_exit(buffer, slot):
        stage, _, _, patch = buffer
        row_at = at_ref[0, slot]
        col_at = at_ref[1, slot]
        tile_at = col_at // LANES
        shift = col_at % LANES
        back_shift = (LANES - shift) % LANES
        lane = lax.broadcasted_iota(jnp.int32, (CHUNK, LANES), 1)
        keep_low = lane < LANES - shift
        for r in range(0, fs, CHUNK):
            rows = slice(r, r + CHUNK)
            values = []
            for plane in range(2):
                rolled = [
                    pltpu.roll(
                        ext_ref[plane, tile_at + t, pl.ds(row_at + r, CHUNK), :], back_shift, 1
                    )
                    for t in range(lane_tiles + 1)
                ]
                values.append(
                    [jnp.where(keep_low, rolled[t], rolled[t + 1]) for t in range(lane_tiles)]
                )
            for t in range(lane_tiles):
                cols = slice(t * LANES, (t + 1) * LANES)
                patch_real, patch_imag = values[0][t], values[1][t]
                patch[0, rows, cols] = patch_real
                patch[1, rows, cols] = patch_imag
                for m in range(modes):
                    probe_real = probe_ref[0, m, rows, cols]
                    probe_imag = probe_ref[1, m, rows, cols]
                    out = slice(m * fs + t * LANES, m * fs + (t + 1) * LANES)
                    stage[rows, out] = (
                        probe_real * patch_real - probe_imag * patch_imag
                    ).astype(jnp.bfloat16)
                    stage[fs + r : fs + r + CHUNK, out] = (
                        probe_real * patch_imag + probe_imag * patch_real
                    ).astype(jnp.bfloat16)

    def make_chi(buffer, slot, valid):
        stage, _, wide, _ = buffer
        for r in range(0, fs, CHUNK):
            for t in range(lane_tiles):
                cols = slice(t * LANES, (t + 1) * LANES)
                imag_cols = slice(fs + t * LANES, fs + (t + 1) * LANES)
                psi = []
                power = None
                for m in range(modes):
                    rows = slice(m * fs + r, m * fs + r + CHUNK)
                    real, imag = wide[rows, cols], wide[rows, imag_cols]
                    psi.append((real, imag))
                    own = real * real + imag * imag
                    power = own if power is None else power + own
                amp = amp_ref[slot, r : r + CHUNK, cols].astype(jnp.float32)
                factor = 1.0 - amp * lax.rsqrt(jnp.maximum(power, 0.25))
                if valid is not None:
                    factor = jnp.where(valid, factor, 0.0)
                for m in range(modes):
                    out = slice(m * fs + t * LANES, m * fs + (t + 1) * LANES)
                    stage[r : r + CHUNK, out] = (psi[m][0] * factor).astype(jnp.bfloat16)
                    stage[fs + r : fs + r + CHUNK, out] = (psi[m][1] * factor).astype(jnp.bfloat16)

    def add_grads(buffer, slot):
        _, _, wide, patch = buffer
        row_at = at_ref[0, slot]
        col_at = at_ref[1, slot]
        tile_at = col_at // LANES
        shift = col_at % LANES
        lane = lax.broadcasted_iota(jnp.int32, (CHUNK, LANES), 1)
        from_same = lane >= shift
        for r in range(0, fs, CHUNK):
            grads = [[], []]
            for t in range(lane_tiles):
                cols = slice(t * LANES, (t + 1) * LANES)
                imag_cols = slice(fs + t * LANES, fs + (t + 1) * LANES)
                patch_real = patch[0, r : r + CHUNK, cols]
                patch_imag = patch[1, r : r + CHUNK, cols]
                total_real = total_imag = None
                for m in range(modes):
                    rows = slice(m * fs + r, m * fs + r + CHUNK)
                    real, imag = wide[rows, cols], wide[rows, imag_cols]
                    probe_real = probe_ref[0, m, r : r + CHUNK, cols]
                    probe_imag = probe_ref[1, m, r : r + CHUNK, cols]
                    own_real = probe_real * real + probe_imag * imag
                    own_imag = probe_real * imag - probe_imag * real
                    total_real = own_real if m == 0 else total_real + own_real
                    total_imag = own_imag if m == 0 else total_imag + own_imag
                    at = (m * lane_tiles + t) * fs + r
                    pacc_ref[at : at + CHUNK, :] += patch_real * real + patch_imag * imag
                    at += modes * lane_tiles * fs
                    pacc_ref[at : at + CHUNK, :] += patch_real * imag - patch_imag * real
                grads[0].append(pltpu.roll(total_real, shift, 1))
                grads[1].append(pltpu.roll(total_imag, shift, 1))
            for plane in range(2):
                rolled = grads[plane]
                for t in range(lane_tiles + 1):
                    same = rolled[t] if t < lane_tiles else 0.0
                    before = rolled[t - 1] if t > 0 else 0.0
                    where = (plane, tile_at + t, pl.ds(row_at + r, CHUNK), slice(None))
                    acc_ref[where] += jnp.where(from_same, same, before)

    def advance(pair, carry):
        first = 2 * pair
        second = jnp.minimum(first + 1, last_slot)
        make_exit(even, first)
        two_sided(even, fwd, inv)
        add_grads(odd, jnp.maximum(first - 1, 0))
        make_exit(odd, second)
        two_sided(odd, fwd, inv)
        make_chi(even, first, None)
        two_sided(even, inv, fwd)
        make_chi(odd, second, first + 1 < live)
        two_sided(odd, inv, fwd)
        add_grads(even, first)
        return carry

    pairs = (live + 1) // 2
    lax.fori_loop(0, pairs, advance, 0)
    add_grads(odd, jnp.minimum(2 * pairs - 1, last_slot))


def frames_call(extended, probe_modes, amplitudes, positions, live_count, tables):
    fs = probe_modes.shape[-1]
    modes = probe_modes.shape[1]
    tiled = extended.shape
    vmem = pl.BlockSpec(memory_space=pltpu.VMEM)
    smem = pl.BlockSpec(memory_space=pltpu.SMEM)
    return pl.pallas_call(
        frames_kernel,
        out_shape=(
            jax.ShapeDtypeStruct(tiled, jnp.float32),
            jax.ShapeDtypeStruct((probe_modes.size // LANES, LANES), jnp.float32),
        ),
        in_specs=[smem, smem, vmem, vmem, vmem, vmem, vmem],
        out_specs=(vmem, vmem),
        scratch_shapes=[
            pltpu.VMEM((2 * fs, 2 * fs), jnp.bfloat16),
            pltpu.VMEM((2 * fs, 2 * fs), jnp.bfloat16),
        ]
        + 2
        * [
            pltpu.VMEM((2 * fs, modes * fs), jnp.bfloat16),
            pltpu.VMEM((modes * fs, 2 * fs), jnp.bfloat16),
            pltpu.VMEM((modes * fs, 2 * fs), jnp.float32),
            pltpu.VMEM((2, fs, fs), jnp.float32),
        ],
        compiler_params=pltpu.CompilerParams(vmem_limit_bytes=26 * 1024 * 1024),
        name="frames",
    )(live_count.reshape(1), positions, extended, probe_modes, amplitudes, *tables)


def shards(object_field, probe_modes, measured_amp, scan_positions, frame_counts):
    slot_count = measured_amp.shape[2]
    extended = halo_call(object_field)
    acc, probe_flat = frames_call(
        extended,
        probe_modes,
        measured_amp[0, 0],
        scan_positions[0, 0],
        frame_counts[0, 0],
        fourier_tables(probe_modes.shape[-1]),
    )
    norm_scale = 1.0 / math.sqrt(lax.axis_size("row") * lax.axis_size("col") * slot_count)
    return reduce_call(acc, probe_flat, object_field.shape, probe_modes.shape, norm_scale)


def solution(mesh):
    in_specs = (
        P(None, "row", "col"),
        P(),
        P("row", "col", None, None, None),
        P("row", "col", None, None),
        P("row", "col"),
    )
    out_specs = (P(None, "row", "col"), P())
    return jax.shard_map(shards, mesh=mesh, in_specs=in_specs, out_specs=out_specs, check_vma=False)
```

profile of v0, /device:TPU:0, one launch (start us, length us, event | category | flops | bytes accessed | tf_op | source)
XLA Modules:
  0.0 58.9 jit_solution(12796271408077137177)
XLA Ops:
  0.6 0.0 copy-start.5
  1.3 0.0 copy-start
  1.3 1.2 %copy-done = bf16[2,512,512]{2,1,0:T(8,128)(2,1)S(1)} copy-done((bf16[2,512,512]{2,1,0:T(8,128)(2,1)S(1)}, bf16[2,512,512]{2,1,0:T(8,128)(2,1)}, u32[]{:S(2)}) %copy-start) | copy-done | bytes 1048600
  2.5 0.0 copy-start.1
  2.5 0.0 copy-start.2
  2.5 0.0 copy-start.3
  2.5 0.0 copy-start.4
  2.5 11.9 %halo.1.ext_ref = f32[2,7,768,128]{3,2,1,0:T(8,128)S(1)} custom-call(bf16[2,512,512]{2,1,0:T(8,128)(2,1)S(1)} %copy-done), custom_call_target="tpu_custom_call" | custom-call | tf_op jit(solution)/shard_map/halo/pallas_call | solution.py:142
  14.4 0.0 copy-done.5
  14.4 0.0 copy-done.1
  14.4 0.0 copy-done.2
  14.4 0.0 copy-done.3
  14.5 0.0 copy-done.4
  14.5 8.0 %frames.1 = (f32[2,7,768,128]{3,2,1,0:T(8,128)S(1)}, f32[2048,128]{1,0:T(8,128)S(1)}) custom-call(s32[1]{0:T(128)} %bitcast.3.count_ref, s32[2,8]{1,0:T(2,128)S(1)} %bitcast.5, f32[2,7,768,128]{3,2,1,0:T(8,128)S(1)} %halo.1.ext_ref, f32[2,2,256,256]{3,2,1,0:T(8,128)S(1)} %copy-done.1, bf16[8,256,256]{2,1,0:T(8,128)(2,1)S(1)} %bitcast.4, ...), custom_call_target="tpu_custom_call" | custom-call | tf_op jit(solution)/shard_map/frames/pallas_call | solution.py:579
  22.5 34.1 %reduce.1 = (f32[2,512,512]{2,1,0:T(8,128)S(1)}, f32[2,2,256,256]{3,2,1,0:T(8,128)S(1)}) custom-call(f32[2,7,768,128]{3,2,1,0:T(8,128)S(1)} %get-tuple-element.4.acc_ref, f32[2048,128]{1,0:T(8,128)S(1)} %get-tuple-element.5.pacc_ref), custom_call_target="tpu_custom_call" | custom-call | tf_op jit(solution)/shard_map/reduce/pallas_call | solution.py:372
  56.6 1.3 %copy.12 = f32[2,512,512]{2,1,0:T(8,128)} copy(f32[2,512,512]{2,1,0:T(8,128)S(1)} %get-tuple-element.8) | data formatting | bytes 4194304
  57.9 1.0 %copy.13 = f32[2,2,256,256]{3,2,1,0:T(8,128)} copy(f32[2,2,256,256]{3,2,1,0:T(8,128)S(1)} %get-tuple-element.9) | data formatting | bytes 2097152
Async XLA Ops:
  0.6 13.8 %copy-start.5 = (s32[1,1,2,8]{3,2,1,0:T(2,128)S(1)}, s32[1,1,2,8]{3,2,1,0:T(2,128)}, u32[]{:S(2)}) copy-start(s32[1,1,2,8]{3,2,1,0:T(2,128)} %param.10) | copy-start | bytes 196
  1.3 1.2 %copy-start = (bf16[2,512,512]{2,1,0:T(8,128)(2,1)S(1)}, bf16[2,512,512]{2,1,0:T(8,128)(2,1)}, u32[]{:S(2)}) copy-start(bf16[2,512,512]{2,1,0:T(8,128)(2,1)} %whole_ref.1) | copy-start | bytes 3145732
  2.5 11.9 %copy-start.1 = (f32[2,2,256,256]{3,2,1,0:T(8,128)S(1)}, f32[2,2,256,256]{3,2,1,0:T(8,128)}, u32[]{:S(2)}) copy-start(f32[2,2,256,256]{3,2,1,0:T(8,128)} %probe_ref.1) | copy-start | bytes 3145732
  2.5 11.9 %copy-start.2 = (bf16[1,1,8,256,256]{4,3,2,1,0:T(8,128)(2,1)S(1)}, bf16[1,1,8,256,256]{4,3,2,1,0:T(8,128)(2,1)}, u32[]{:S(2)}) copy-start(bf16[1,1,8,256,256]{4,3,2,1,0:T(8,128)(2,1)} %param.9) | copy-start | bytes 3145732
  2.5 11.9 %copy-start.3 = (bf16[256,256]{1,0:T(8,128)(2,1)S(1)}, bf16[256,256]{1,0:T(8,128)(2,1)}, u32[]{:S(2)}) copy-start(bf16[256,256]{1,0:T(8,128)(2,1)} %constant.10.ti_ref) | copy-start | bytes 393220
  2.5 11.9 %copy-start.4 = (bf16[256,256]{1,0:T(8,128)(2,1)S(1)}, bf16[256,256]{1,0:T(8,128)(2,1)}, u32[]{:S(2)}) copy-start(bf16[256,256]{1,0:T(8,128)(2,1)} %constant.9.tr_ref) | copy-start | bytes 393220
where the time goes:
time: 58.9 us
  Pallas kernels  54 us (92%)
  local copies, waits for them, and re-layouts  3.53 us (6%)
  between operations  1.37 us (2%)
    pallas_call x1, Pallas kernels, reduce_call(): pl.pallas_call(functools.partial(reduce_kernel, scale), out_shape=(jax.Sh...  34.1 us
    pallas_call x1, Pallas kernels, halo_call(): pl.pallas_call(halo_kernel, out_shape=jax.ShapeDtypeStruct((2, (side_cols...  11.9 us
    pallas_call x1, Pallas kernels, frames_call(): pl.pallas_call(frames_kernel, out_shape=(jax.ShapeDtypeStruct(tiled, jnp....  8.01 us
    unnamed x14, local copies, waits for them, and re-layouts  3.53 us

commit v1 on v0

v1 whole, which is shorter than its diff:
```python
import functools
import math

import jax
import jax.numpy as jnp
import numpy as np
from jax import lax
from jax.experimental import pallas as pl
from jax.experimental.pallas import tpu as pltpu
from jax.sharding import PartitionSpec as P

HALO = 128
LANES = 128
PARTS = 2
HALO_LIMIT = 20


MESH = pl.DeviceIdType.MESH
SIDES = [(dr, dc) for dr in (-1, 0, 1) for dc in (-1, 0, 1) if (dr, dc) != (0, 0)]


def position():
    return (
        lax.axis_index("row"),
        lax.axis_index("col"),
        lax.axis_size("row"),
        lax.axis_size("col"),
    )


def exists(side):
    row, col, rows, cols = position()
    dr, dc = side
    inside = jnp.bool_(True)
    if dr:
        inside = row + dr >= 0 if dr < 0 else row + dr < rows
    if dc:
        other = col + dc >= 0 if dc < 0 else col + dc < cols
        inside = jnp.logical_and(inside, other) if dr else other
    return inside


def at_side(side):
    row, col, _, _ = position()
    return (row + side[0], col + side[1])


def opposite(side):
    return (-side[0], -side[1])


def part(step, margin, inner):
    return {-1: slice(0, margin), 0: slice(margin, margin + inner), 1: slice(margin + inner, None)}[
        step
    ]


def edge(step, margin, inner):
    return {-1: slice(0, margin), 0: slice(0, inner), 1: slice(inner - margin, inner)}[step]


def to_side(side, index, source, landing, send_sems, recv_sems):
    return pltpu.make_async_remote_copy(
        src_ref=source,
        dst_ref=landing,
        send_sem=send_sems.at[index],
        recv_sem=recv_sems.at[index],
        device_id=at_side(side),
        device_id_type=MESH,
    )


DIRECT = 1


def halo_kernel(whole_ref, ext_ref, acc_ref, pacc_ref, *scratch):
    object_ref, load_sem, row_land, col_land, corner_land, relay_land = scratch[:6]
    row_sems, col_sems, corner_sems, relay_sems = scratch[6:]
    row, col, n_row, n_col = position()
    side_rows, side_cols = object_ref.shape[1:]
    load = pltpu.make_async_copy(whole_ref, object_ref, load_sem)
    load.start()
    steps = (-1, 1)
    pieces = (slice(0, HALO), slice(side_cols - HALO, side_cols), slice(HALO, side_cols - HALO))
    direct = DIRECT * side_rows // 4
    parts = (slice(0, direct), slice(direct, side_rows))

    def has(dr, dc):
        return exists((dr, dc))

    def turns(d):
        return jnp.logical_and(has(0, d), lax.rem(col, 4) == (3 if d > 0 else 0))

    def relays(d):
        other = col - 3 * d
        inside = jnp.logical_and(other >= 0, other < n_col)
        return jnp.logical_and(inside, lax.rem(col, 4) == (2 if d > 0 else 1))

    def lands_by_relay(d):
        return jnp.logical_and(has(0, -d), lax.rem(col, 4) == (0 if d > 0 else 3))

    links = []
    for d in steps:
        links.append((has(d, 0), (row + d, col)))
        links.append((has(0, d), (row, col + d)))
        links.append((turns(d), (row, col + 3 * d)))
        links.append((relays(d), (row, col - 3 * d)))
        links.append((relays(d), (row, col - 2 * d)))
        links.append((lands_by_relay(d), (row, col + 2 * d)))
    barrier = pltpu.get_barrier_semaphore()
    count = jnp.int32(0)
    for there, device in links:

        @pl.when(there)
        def _(device=device):
            pl.semaphore_signal(barrier, inc=1, device_id=device, device_id_type=MESH)

        count = count + there.astype(jnp.int32)
    pl.semaphore_wait(barrier, count)

    def remote(source, landing, sems, index, device):
        return pltpu.make_async_remote_copy(
            src_ref=source,
            dst_ref=landing,
            send_sem=sems.at[0, index],
            recv_sem=sems.at[1, index],
            device_id=device,
            device_id_type=MESH,
        )

    def row_copy(s, p):
        d = steps[s]
        source = whole_ref.at[:, edge(d, HALO, side_rows), pieces[p]]
        return remote(
            source, row_land.at[1 - s, :, :, pieces[p]], row_sems, 3 * s + p, (row + d, col)
        )

    def col_copy(s, p, to_relay=False):
        d = steps[s]
        source = whole_ref.at[:, parts[p], edge(d, HALO, side_cols)]
        if to_relay:
            return pltpu.make_async_remote_copy(
                src_ref=source,
                dst_ref=relay_land.at[s],
                send_sem=col_sems.at[0, 2 * s + p],
                recv_sem=relay_sems.at[1, s],
                device_id=(row, col + 3 * d),
                device_id_type=MESH,
            )
        return remote(
            source, col_land.at[1 - s, :, parts[p], :], col_sems, 2 * s + p, (row, col + d)
        )

    def relay_copy(s):
        d = steps[s]
        return pltpu.make_async_remote_copy(
            src_ref=relay_land.at[s],
            dst_ref=col_land.at[1 - s, :, parts[1], :],
            send_sem=relay_sems.at[0, s],
            recv_sem=col_sems.at[1, 2 * s + 1],
            device_id=(row, col - 2 * d),
            device_id_type=MESH,
        )

    def corner_copy(r, s):
        source = row_land.at[r, :, :, pieces[s]]
        return remote(
            source, corner_land.at[r, 1 - s], corner_sems, 2 * r + s, (row, col + steps[s])
        )

    def when(condition, action):
        @pl.when(condition)
        def _():
            action()

    for p in range(2):
        for s, d in enumerate(steps):
            when(has(d, 0), lambda s=s, p=p: row_copy(s, p).start())
    for p in (1, 0):
        for s, d in enumerate(steps):
            if p:
                when(turns(d), lambda s=s: col_copy(s, 1, True).start())
                straight = jnp.logical_and(has(0, d), jnp.logical_not(turns(d)))
                when(straight, lambda s=s: col_copy(s, 1).start())
            else:
                when(has(0, d), lambda s=s: col_copy(s, 0).start())
    for s, d in enumerate(steps):
        when(has(d, 0), lambda s=s: row_copy(s, 2).start())

    acc_ref[...] = jnp.zeros(acc_ref.shape, jnp.float32)
    pacc_ref[...] = jnp.zeros(pacc_ref.shape, jnp.float32)
    spare = ext_ref.shape[1] - 1
    ext_ref[:, spare] = jnp.zeros((2, ext_ref.shape[2], LANES), jnp.float32)
    margin, inner = HALO // LANES, side_cols // LANES

    def tiles_of(d):
        return range(spare)[part(d, margin, inner)]

    def fill(rows, tiles, height, source):
        for k, t in enumerate(tiles):
            if source is None:
                ext_ref[:, t, rows, :] = jnp.zeros((2, height, LANES), ext_ref.dtype)
            else:
                ext_ref[:, t, rows, :] = source[:, :, k * LANES : (k + 1) * LANES].astype(
                    jnp.float32
                )

    load.wait()
    fill(part(0, HALO, side_rows), tiles_of(0), side_rows, object_ref)

    for s, d in enumerate(steps):

        def pass_on(s=s):
            relay_copy_in = col_copy(s, 1, True)
            relay_copy_in.wait_recv()
            relay_copy(s).start()

        when(relays(d), pass_on)
    for r, dr in enumerate(steps):
        for s, dc in enumerate(steps):

            def hand_over(r=r, s=s, dc=dc):
                row_copy(1 - r, s).wait_recv()
                when(has(0, dc), lambda: corner_copy(r, s).start())

            when(has(dr, 0), hand_over)
    for s, d in enumerate(steps):
        rows = part(0, HALO, side_rows)
        here = s

        def take(s=s, d=d, rows=rows):
            col_copy(1 - s, 0).wait_recv()
            col_copy(1 - s, 1).wait_recv()
            fill(rows, tiles_of(d), side_rows, col_land.at[s])

        when(has(0, d), take)
        when(
            jnp.logical_not(has(0, d)), lambda d=d, rows=rows: fill(rows, tiles_of(d), side_rows, None)
        )
    for r, dr in enumerate(steps):
        rows = part(dr, HALO, side_rows)

        def take_rows(r=r, rows=rows):
            row_copy(1 - r, 2).wait_recv()
            fill(rows, tiles_of(0), HALO, row_land.at[r])

        when(has(dr, 0), take_rows)
        when(
            jnp.logical_not(has(dr, 0)), lambda rows=rows: fill(rows, tiles_of(0), HALO, None)
        )
    for r, dr in enumerate(steps):
        rows = part(dr, HALO, side_rows)
        for s, dc in enumerate(steps):

            def take_corner(r=r, s=s, dc=dc, rows=rows):
                corner_copy(r, 1 - s).wait_recv()
                fill(rows, tiles_of(dc), HALO, corner_land.at[r, s])

            when(has(dr, dc), take_corner)
            when(
                jnp.logical_not(has(dr, dc)),
                lambda dc=dc, rows=rows: fill(rows, tiles_of(dc), HALO, None),
            )

    for s, d in enumerate(steps):
        for p in range(3):
            when(has(d, 0), lambda s=s, p=p: row_copy(s, p).wait_send())
        for p in range(2):
            when(has(0, d), lambda s=s, p=p: col_copy(s, p).wait_send())
        when(relays(d), lambda s=s: relay_copy(s).wait_send())
        for r, dr in enumerate(steps):
            when(has(dr, d), lambda r=r, s=s: corner_copy(r, s).wait_send())


def halo_call(object_field, probe_size):
    planes, side_rows, side_cols = object_field.shape
    kind = object_field.dtype
    vmem = pl.BlockSpec(memory_space=pltpu.VMEM)
    tiled = jax.ShapeDtypeStruct(
        (planes, (side_cols + 2 * HALO) // LANES + 1, side_rows + 2 * HALO, LANES), jnp.float32
    )
    direct = DIRECT * side_rows // 4
    return pl.pallas_call(
        halo_kernel,
        out_shape=(tiled, tiled, jax.ShapeDtypeStruct((probe_size // LANES, LANES), jnp.float32)),
        in_specs=[pl.BlockSpec(memory_space=pltpu.HBM)],
        out_specs=(vmem, vmem, vmem),
        scratch_shapes=[
            pltpu.VMEM(object_field.shape, kind),
            pltpu.SemaphoreType.DMA,
            pltpu.VMEM((2, planes, HALO, side_cols), kind),
            pltpu.VMEM((2, planes, side_rows, HALO), kind),
            pltpu.VMEM((2, 2, planes, HALO, HALO), kind),
            pltpu.VMEM((2, planes, side_rows - direct, HALO), kind),
            pltpu.SemaphoreType.DMA((2, 6)),
            pltpu.SemaphoreType.DMA((2, 4)),
            pltpu.SemaphoreType.DMA((2, 4)),
            pltpu.SemaphoreType.DMA((2, 2)),
        ],
        compiler_params=pltpu.CompilerParams(
            collective_id=0, has_side_effects=True, vmem_limit_bytes=HALO_LIMIT * 1024 * 1024
        ),
        cost_estimate=pl.CostEstimate(flops=10**10, bytes_accessed=0, transcendentals=0),
        name="halo",
    )(pltpu.with_memory_space_constraint(object_field, pltpu.HBM))


def reduce_kernel(scale, acc_ref, pacc_ref, grad_ref, probe_ref, *scratch):
    count = len(SIDES)
    sends, landings, rest = scratch[:count], scratch[count : 2 * count], scratch[2 * count :]
    psend, pair_recv, merged, precv, sums, zbuf, full = rest[:7]
    side_sems, pair_sems, col_sems, row_sems = rest[7:]
    row, col, n_row, n_col = position()
    side_rows, side_cols = grad_ref.shape[1:]
    margin = HALO // LANES
    inner = side_cols // LANES
    part_rows = psend.shape[2]
    share = PARTS * part_rows
    chip, core = col // 2, lax.rem(col, 2)
    n_chip = n_col // 2
    sibling = (row, 2 * chip + 1 - core)

    barrier = pltpu.get_barrier_semaphore()
    waits = jnp.int32(n_row + n_chip - 1)
    pl.semaphore_signal(barrier, inc=1, device_id=sibling, device_id_type=MESH)
    for k in range(1, n_chip):
        peer = (row, 2 * lax.rem(chip + k, n_chip) + core)
        pl.semaphore_signal(barrier, inc=1, device_id=peer, device_id_type=MESH)
    for k in range(1, n_row):
        pl.semaphore_signal(
            barrier, inc=1, device_id=(lax.rem(row + k, n_row), col), device_id_type=MESH
        )
    for side in SIDES:
        if side[1]:

            @pl.when(exists(side))
            def _(side=side):
                pl.semaphore_signal(barrier, inc=1, device_id=at_side(side), device_id_type=MESH)

            waits = waits + exists(side).astype(jnp.int32)

    def stage_side(index):
        dr, dc = SIDES[index]
        tiles = range(inner + 2 * margin)[part(dc, margin, inner)]
        for k, t in enumerate(tiles):
            sends[index][:, k] = acc_ref[:, t, part(dr, HALO, side_rows), :].astype(jnp.bfloat16)

    def stage_sides(chosen):
        for index, side in enumerate(SIDES):
            if chosen(side):
                stage_side(index)

    def to_peer(source, landing, sems, which, k, device):
        return pltpu.make_async_remote_copy(
            src_ref=source,
            dst_ref=landing,
            send_sem=sems.at[which, k],
            recv_sem=sems.at[which + 1, k],
            device_id=device,
            device_id_type=MESH,
        )

    def chip_at(k):
        return lax.rem(chip + k, n_chip)

    def chip_from(k):
        return lax.rem(chip + n_chip - k, n_chip)

    def chip_peer(k):
        return (row, 2 * chip_at(k) + core)

    def rows_of(index, h):
        return pl.ds(pl.multiple_of(index * share + h * part_rows, part_rows), part_rows)

    def pair_copy(h, k):
        return to_peer(
            psend.at[h, k], pair_recv.at[h, k], pair_sems, 0, h * n_chip + k, sibling
        )

    def scatter_copy(h, k):
        at = h * (n_chip - 1) + k - 1
        return to_peer(merged.at[h, k - 1], precv.at[h, k - 1], col_sems, 0, at, chip_peer(k))

    def row_copy(h, k, owner):
        at = h * (n_row - 1) + k - 1
        peer = (lax.rem(row + k, n_row), col)
        return to_peer(zbuf.at[h, row], zbuf.at[h, owner], row_sems, 0, at, peer)

    def gather_copy(h, k, owner):
        at = h * (n_chip - 1) + k - 1
        source, landing = full.at[rows_of(col, h), :], full.at[rows_of(owner, h), :]
        return to_peer(source, landing, col_sems, 2, at, chip_peer(k))

    def forward_copy(h, k, side):
        source = full.at[rows_of(2 * chip_from(k) + core, h), :]
        landing = full.at[rows_of(2 * chip_from(k) + side, h), :]
        return to_peer(source, landing, pair_sems, 2, h * n_chip + k, sibling)

    def side_copy(index):
        return to_side(
            SIDES[index], index, sends[index], landings[index], side_sems.at[0], side_sems.at[1]
        )

    def start_sides(chosen):
        for index, side in enumerate(SIDES):
            if chosen(side):

                @pl.when(exists(side))
                def _(index=index):
                    side_copy(index).start()

    def add_sides(chosen):
        for index, side in enumerate(SIDES):
            if not chosen(side):
                continue
            dr, dc = opposite(side)
            rows = edge(dr, HALO, side_rows)
            tiles = range(inner)[edge(dc, margin, inner)]

            @pl.when(exists((dr, dc)))
            def _(index=index, rows=rows, tiles=tiles):
                side_copy(index).wait_recv()
                for k, t in enumerate(tiles):
                    grad_ref[:, rows, t * LANES : (t + 1) * LANES] += landings[index][
                        :, k
                    ].astype(jnp.float32)

    over_rows = lambda side: side[1] == 0
    over_cols = lambda side: side[0] == 0
    corners = lambda side: side[0] != 0 and side[1] != 0
    order = list(range(1, n_chip)) + [0]
    for h in range(PARTS):
        for k in order:
            psend[h, k] = pacc_ref[rows_of(2 * chip_at(k) + 1 - core, h), :].astype(jnp.bfloat16)
    stage_sides(over_rows)
    pl.semaphore_wait(barrier, waits)
    for h in range(PARTS):
        for k in order:
            pair_copy(h, k).start()
    start_sides(over_rows)
    stage_sides(over_cols)
    stage_sides(corners)

    def merge(h, k):
        pair_copy(h, k).wait_recv()
        own = pacc_ref[rows_of(2 * chip_at(k) + core, h), :]
        return own + pair_recv[h, k].astype(jnp.float32)

    for h in range(PARTS):
        for k in range(1, n_chip):
            merged[h, k - 1] = merge(h, k).astype(jnp.bfloat16)
            scatter_copy(h, k).start()
        sums[h] = merge(h, 0)
    start_sides(over_cols)
    for t in range(inner):
        grad_ref[:, :, t * LANES : (t + 1) * LANES] = acc_ref[
            :, margin + t, HALO : HALO + side_rows, :
        ]
    for h in range(PARTS):
        total = sums[h]
        for k in range(1, n_chip):
            scatter_copy(h, k).wait_recv()
            total = total + precv[h, k - 1].astype(jnp.float32)
        zbuf[h, row] = total.astype(jnp.bfloat16)
        for k in range(1, n_row):
            row_copy(h, k, row).start()
    start_sides(corners)
    for h in range(PARTS):
        for k in range(1, n_row):
            row_copy(h, k, lax.rem(row + n_row - k, n_row)).wait_recv()
        total = zbuf[h, 0].astype(jnp.float32)
        for k in range(1, n_row):
            total = total + zbuf[h, k].astype(jnp.float32)
        full[rows_of(col, h), :] = (total * scale).astype(jnp.bfloat16)
        for k in range(1, n_chip):
            gather_copy(h, k, col).start()
        forward_copy(h, 0, core).start()
    add_sides(over_rows)
    add_sides(over_cols)
    for h in range(PARTS):
        for k in range(1, n_chip):
            gather_copy(h, k, 2 * chip_from(k) + core).wait_recv()
            forward_copy(h, k, core).start()
    add_sides(corners)

    for h in range(PARTS):
        for k in range(n_chip):
            forward_copy(h, k, 1 - core).wait_recv()
    parts, modes, fs, width = probe_ref.shape
    at = 0
    for p in range(parts):
        for m in range(modes):
            for t in range(width // LANES):
                probe_ref[p, m, :, t * LANES : (t + 1) * LANES] = full[at : at + fs, :].astype(
                    jnp.float32
                )
                at += fs
    for h in range(PARTS):
        for k in range(1, n_chip):
            scatter_copy(h, k).wait_send()
            gather_copy(h, k, col).wait_send()
        for k in range(n_chip):
            pair_copy(h, k).wait_send()
            forward_copy(h, k, core).wait_send()
        for k in range(1, n_row):
            row_copy(h, k, row).wait_send()
    for index, side in enumerate(SIDES):

        @pl.when(exists(side))
        def _(index=index):
            side_copy(index).wait_send()


def reduce_call(acc, probe_flat, object_shape, probe_shape, scale):
    n_row, n_col = lax.axis_size("row"), lax.axis_size("col")
    _, side_rows, side_cols = object_shape
    inner = side_cols // LANES
    margin = HALO // LANES
    vmem = pl.BlockSpec(memory_space=pltpu.VMEM)
    buffers = []
    for dr, dc in SIDES:
        buffers.append(
            pltpu.VMEM(
                (2, margin if dc else inner, HALO if dr else side_rows, LANES), jnp.bfloat16
            )
        )
    total_rows = probe_flat.shape[0]
    piece = total_rows // n_col // PARTS
    n_chip = n_col // 2
    return pl.pallas_call(
        functools.partial(reduce_kernel, scale),
        out_shape=(
            jax.ShapeDtypeStruct(object_shape, jnp.float32),
            jax.ShapeDtypeStruct(probe_shape, jnp.float32),
        ),
        in_specs=[vmem, vmem],
        out_specs=(vmem, vmem),
        scratch_shapes=buffers
        + buffers
        + [
            pltpu.VMEM((PARTS, n_chip, piece, LANES), jnp.bfloat16),
            pltpu.VMEM((PARTS, n_chip, piece, LANES), jnp.bfloat16),
            pltpu.VMEM((PARTS, n_chip - 1, piece, LANES), jnp.bfloat16),
            pltpu.VMEM((PARTS, n_chip - 1, piece, LANES), jnp.bfloat16),
            pltpu.VMEM((PARTS, piece, LANES), jnp.float32),
            pltpu.VMEM((PARTS, n_row, piece, LANES), jnp.bfloat16),
            pltpu.VMEM((total_rows, LANES), jnp.bfloat16),
            pltpu.SemaphoreType.DMA((2, len(SIDES))),
            pltpu.SemaphoreType.DMA((4, PARTS * n_chip)),
            pltpu.SemaphoreType.DMA((4, PARTS * (n_chip - 1))),
            pltpu.SemaphoreType.DMA((2, PARTS * (n_row - 1))),
        ],
        compiler_params=pltpu.CompilerParams(
            collective_id=1, has_side_effects=True, vmem_limit_bytes=20 * 1024 * 1024
        ),
        name="reduce",
    )(acc, probe_flat)


def fourier_tables(frame_side):
    indices = np.arange(frame_side)
    product = indices[:, None] * indices[None, :] % frame_side
    angles = 2.0 * math.pi / frame_side * product
    norm_scale = 1.0 / math.sqrt(frame_side)
    real, imag = np.cos(angles) * norm_scale, -np.sin(angles) * norm_scale
    tables = (np.block([[real, -imag], [imag, real]]), np.block([[real, imag], [-imag, real]]))
    return tuple(jnp.asarray(table.astype(np.float32)).astype(jnp.bfloat16) for table in tables)


CHUNK = 32


def dot32(left, right):
    return jnp.dot(left, right, preferred_element_type=jnp.float32)


def frames_kernel(
    count_ref, at_ref, ext_ref, probe_ref, amp_ref, fwd, inv, zero_ref, pzero_ref,
    acc_ref, pacc_ref, *buffers,
):
    fs = probe_ref.shape[-1]
    modes = probe_ref.shape[1]
    lane_tiles = fs // LANES
    last_slot = amp_ref.shape[0] - 1
    live = count_ref[0]
    even, odd = buffers[:4], buffers[4:]
    odd[2][...] = jnp.zeros(odd[2].shape, jnp.float32)
    odd[3][...] = jnp.zeros(odd[3].shape, jnp.float32)

    def two_sided(buffer, left_table, right_table):
        stage, half, wide, _ = buffer
        for m in range(modes):
            both = dot32(left_table[...], stage[:, m * fs : (m + 1) * fs])
            half[m * fs : (m + 1) * fs, :fs] = both[:fs].astype(jnp.bfloat16)
            half[m * fs : (m + 1) * fs, fs:] = both[fs:].astype(jnp.bfloat16)
        wide[...] = dot32(half[...], right_table[...])

    def make_exit(buffer, slot):
        stage, _, _, patch = buffer
        row_at = at_ref[0, slot]
        col_at = at_ref[1, slot]
        tile_at = col_at // LANES
        shift = col_at % LANES
        back_shift = (LANES - shift) % LANES
        lane = lax.broadcasted_iota(jnp.int32, (CHUNK, LANES), 1)
        keep_low = lane < LANES - shift
        for r in range(0, fs, CHUNK):
            rows = slice(r, r + CHUNK)
            values = []
            for plane in range(2):
                rolled = [
                    pltpu.roll(
                        ext_ref[plane, tile_at + t, pl.ds(row_at + r, CHUNK), :], back_shift, 1
                    )
                    for t in range(lane_tiles + 1)
                ]
                values.append(
                    [jnp.where(keep_low, rolled[t], rolled[t + 1]) for t in range(lane_tiles)]
                )
            for t in range(lane_tiles):
                cols = slice(t * LANES, (t + 1) * LANES)
                patch_real, patch_imag = values[0][t], values[1][t]
                patch[0, rows, cols] = patch_real
                patch[1, rows, cols] = patch_imag
                for m in range(modes):
                    probe_real = probe_ref[0, m, rows, cols]
                    probe_imag = probe_ref[1, m, rows, cols]
                    out = slice(m * fs + t * LANES, m * fs + (t + 1) * LANES)
                    stage[rows, out] = (
                        probe_real * patch_real - probe_imag * patch_imag
                    ).astype(jnp.bfloat16)
                    stage[fs + r : fs + r + CHUNK, out] = (
                        probe_real * patch_imag + probe_imag * patch_real
                    ).astype(jnp.bfloat16)

    def make_chi(buffer, slot, valid):
        stage, _, wide, _ = buffer
        for r in range(0, fs, CHUNK):
            for t in range(lane_tiles):
                cols = slice(t * LANES, (t + 1) * LANES)
                imag_cols = slice(fs + t * LANES, fs + (t + 1) * LANES)
                psi = []
                power = None
                for m in range(modes):
                    rows = slice(m * fs + r, m * fs + r + CHUNK)
                    real, imag = wide[rows, cols], wide[rows, imag_cols]
                    psi.append((real, imag))
                    own = real * real + imag * imag
                    power = own if power is None else power + own
                amp = amp_ref[slot, r : r + CHUNK, cols].astype(jnp.float32)
                factor = 1.0 - amp * lax.rsqrt(jnp.maximum(power, 0.25))
                if valid is not None:
                    factor = jnp.where(valid, factor, 0.0)
                for m in range(modes):
                    out = slice(m * fs + t * LANES, m * fs + (t + 1) * LANES)
                    stage[r : r + CHUNK, out] = (psi[m][0] * factor).astype(jnp.bfloat16)
                    stage[fs + r : fs + r + CHUNK, out] = (psi[m][1] * factor).astype(jnp.bfloat16)

    def add_grads(buffer, slot):
        _, _, wide, patch = buffer
        row_at = at_ref[0, slot]
        col_at = at_ref[1, slot]
        tile_at = col_at // LANES
        shift = col_at % LANES
        lane = lax.broadcasted_iota(jnp.int32, (CHUNK, LANES), 1)
        from_same = lane >= shift
        for r in range(0, fs, CHUNK):
            grads = [[], []]
            for t in range(lane_tiles):
                cols = slice(t * LANES, (t + 1) * LANES)
                imag_cols = slice(fs + t * LANES, fs + (t + 1) * LANES)
                patch_real = patch[0, r : r + CHUNK, cols]
                patch_imag = patch[1, r : r + CHUNK, cols]
                total_real = total_imag = None
                for m in range(modes):
                    rows = slice(m * fs + r, m * fs + r + CHUNK)
                    real, imag = wide[rows, cols], wide[rows, imag_cols]
                    probe_real = probe_ref[0, m, r : r + CHUNK, cols]
                    probe_imag = probe_ref[1, m, r : r + CHUNK, cols]
                    own_real = probe_real * real + probe_imag * imag
                    own_imag = probe_real * imag - probe_imag * real
                    total_real = own_real if m == 0 else total_real + own_real
                    total_imag = own_imag if m == 0 else total_imag + own_imag
                    at = (m * lane_tiles + t) * fs + r
                    pacc_ref[at : at + CHUNK, :] += patch_real * real + patch_imag * imag
                    at += modes * lane_tiles * fs
                    pacc_ref[at : at + CHUNK, :] += patch_real * imag - patch_imag * real
                grads[0].append(pltpu.roll(total_real, shift, 1))
                grads[1].append(pltpu.roll(total_imag, shift, 1))
            for plane in range(2):
                rolled = grads[plane]
                for t in range(lane_tiles + 1):
                    same = rolled[t] if t < lane_tiles else 0.0
                    before = rolled[t - 1] if t > 0 else 0.0
                    where = (plane, tile_at + t, pl.ds(row_at + r, CHUNK), slice(None))
                    acc_ref[where] += jnp.where(from_same, same, before)

    def advance(pair, carry):
        first = 2 * pair
        second = jnp.minimum(first + 1, last_slot)
        make_exit(even, first)
        two_sided(even, fwd, inv)
        add_grads(odd, jnp.maximum(first - 1, 0))
        make_exit(odd, second)
        two_sided(odd, fwd, inv)
        make_chi(even, first, None)
        two_sided(even, inv, fwd)
        make_chi(odd, second, first + 1 < live)
        two_sided(odd, inv, fwd)
        add_grads(even, first)
        return carry

    pairs = (live + 1) // 2
    lax.fori_loop(0, pairs, advance, 0)
    add_grads(odd, jnp.minimum(2 * pairs - 1, last_slot))


def frames_call(extended, zeros, probe_modes, amplitudes, positions, live_count, tables):
    fs = probe_modes.shape[-1]
    modes = probe_modes.shape[1]
    tiled = extended.shape
    vmem = pl.BlockSpec(memory_space=pltpu.VMEM)
    smem = pl.BlockSpec(memory_space=pltpu.SMEM)
    return pl.pallas_call(
        frames_kernel,
        out_shape=(
            jax.ShapeDtypeStruct(tiled, jnp.float32),
            jax.ShapeDtypeStruct((probe_modes.size // LANES, LANES), jnp.float32),
        ),
        in_specs=[smem, smem] + 7 * [vmem],
        out_specs=(vmem, vmem),
        input_output_aliases={7: 0, 8: 1},
        scratch_shapes=2
        * [
            pltpu.VMEM((2 * fs, modes * fs), jnp.bfloat16),
            pltpu.VMEM((modes * fs, 2 * fs), jnp.bfloat16),
            pltpu.VMEM((modes * fs, 2 * fs), jnp.float32),
            pltpu.VMEM((2, fs, fs), jnp.float32),
        ],
        compiler_params=pltpu.CompilerParams(vmem_limit_bytes=26 * 1024 * 1024),
        name="frames",
    )(live_count.reshape(1), positions, extended, probe_modes, amplitudes, *tables, *zeros)


def shards(object_field, probe_modes, measured_amp, scan_positions, frame_counts):
    slot_count = measured_amp.shape[2]
    extended, *zeros = halo_call(object_field, probe_modes.size)
    acc, probe_flat = frames_call(
        extended,
        zeros,
        probe_modes,
        measured_amp[0, 0],
        scan_positions[0, 0],
        frame_counts[0, 0],
        fourier_tables(probe_modes.shape[-1]),
    )
    norm_scale = 1.0 / math.sqrt(lax.axis_size("row") * lax.axis_size("col") * slot_count)
    return reduce_call(acc, probe_flat, object_field.shape, probe_modes.shape, norm_scale)


def solution(mesh):
    in_specs = (
        P(None, "row", "col"),
        P(),
        P("row", "col", None, None, None),
        P("row", "col", None, None),
        P("row", "col"),
    )
    out_specs = (P(None, "row", "col"), P())
    return jax.shard_map(shards, mesh=mesh, in_specs=in_specs, out_specs=out_specs, check_vma=False)
```

time: 58.9 us -> 52.3 us (0.89)
  Pallas kernels: 54 us -> 48.6 us
  local copies, waits for them, and re-layouts: 3.53 us -> 2.32 us
    pallas_call x1, Pallas kernels: 34.1 us -> 29.3 us  [reduce_call(): pl.pallas_call(functools.partial(reduce_kernel, scale), out_shape=(jax.Sh...]
    unnamed x14 -> x12, local copies, waits for them, and re-layouts: 3.53 us -> 2.32 us
where the time goes in v1:
time: 52.3 us
  Pallas kernels  48.6 us (93%)
  local copies, waits for them, and re-layouts  2.32 us (4%)
  between operations  1.37 us (3%)
    pallas_call x1, Pallas kernels, reduce_call(): pl.pallas_call(functools.partial(reduce_kernel, scale), out_shape=(jax.Sh...  29.3 us
    pallas_call x1, Pallas kernels, halo_call(): pl.pallas_call(halo_kernel, out_shape=(tiled, tiled, jax.ShapeDtypeStruct...  11.8 us
    pallas_call x1, Pallas kernels, frames_call(): pl.pallas_call(frames_kernel, out_shape=(jax.ShapeDtypeStruct(tiled, jnp....  7.49 us
    unnamed x12, local copies, waits for them, and re-layouts  2.32 us

profile of v1, /device:TPU:0, one launch (start us, length us, event | category | flops | bytes accessed | tf_op | source)
XLA Modules:
  0.0 52.3 jit_solution(1244945568527772555)
XLA Ops:
  1.3 0.0 copy-start
  1.3 0.0 copy-start.1
  1.3 0.0 copy-start.2
  1.3 0.0 copy-start.3
  1.3 0.0 copy-start.4
  1.3 11.8 %halo.1 = (f32[2,7,768,128]{3,2,1,0:T(8,128)S(1)}, f32[2,7,768,128]{3,2,1,0:T(8,128)S(1)}, f32[2048,128]{1,0:T(8,128)S(1)}) custom-call(bf16[2,512,512]{2,1,0:T(8,128)(2,1)} %whole_ref.1), custom_call_target="tpu_custom_call" | custom-call | flops 10000000000 | tf_op jit(solution)/shard_map/halo/pallas_call | solution.py:283
  13.2 0.0 copy-done
  13.2 0.0 copy-done.1
  13.2 0.0 copy-done.2
  13.2 0.0 copy-done.3
  13.2 0.0 copy-done.4
  13.2 7.5 %frames.1 = (f32[2,7,768,128]{3,2,1,0:T(8,128)S(1)}, f32[2048,128]{1,0:T(8,128)S(1)}) custom-call(s32[1]{0:T(128)} %bitcast.3.count_ref, s32[2,8]{1,0:T(2,128)S(1)} %bitcast.5, f32[2,7,768,128]{3,2,1,0:T(8,128)S(1)} %get-tuple-element.7.ext_ref, f32[2,2,256,256]{3,2,1,0:T(8,128)S(1)} %copy-done, ...), custom_call_target="tpu_custom_call", output_to_operand_aliasing={{0}: (7, {}), {1}: (8, {})} | custom-call | tf_op jit(solution)/shard_map/frames/pallas_call | solution.py:724
  20.7 29.3 %reduce.1 = (f32[2,512,512]{2,1,0:T(8,128)S(1)}, f32[2,2,256,256]{3,2,1,0:T(8,128)S(1)}) custom-call(f32[2,7,768,128]{3,2,1,0:T(8,128)S(1)} %get-tuple-element.10.acc_ref, f32[2048,128]{1,0:T(8,128)S(1)} %get-tuple-element.11.pacc_ref), custom_call_target="tpu_custom_call" | custom-call | tf_op jit(solution)/shard_map/reduce/pallas_call | solution.py:530
  50.0 1.3 %copy.16 = f32[2,512,512]{2,1,0:T(8,128)} copy(f32[2,512,512]{2,1,0:T(8,128)S(1)} %get-tuple-element.14) | data formatting | bytes 4194304
  51.3 1.0 %copy.17 = f32[2,2,256,256]{3,2,1,0:T(8,128)} copy(f32[2,2,256,256]{3,2,1,0:T(8,128)S(1)} %get-tuple-element.15) | data formatting | bytes 2097152
Async XLA Ops:
  1.3 11.9 %copy-start = (f32[2,2,256,256]{3,2,1,0:T(8,128)S(1)}, f32[2,2,256,256]{3,2,1,0:T(8,128)}, u32[]{:S(2)}) copy-start(f32[2,2,256,256]{3,2,1,0:T(8,128)} %probe_ref.1) | copy-start | bytes 3145732
  1.3 11.9 %copy-start.1 = (bf16[1,1,8,256,256]{4,3,2,1,0:T(8,128)(2,1)S(1)}, bf16[1,1,8,256,256]{4,3,2,1,0:T(8,128)(2,1)}, u32[]{:S(2)}) copy-start(bf16[1,1,8,256,256]{4,3,2,1,0:T(8,128)(2,1)} %param.9) | copy-start | bytes 3145732
  1.3 11.9 %copy-start.2 = (bf16[512,512]{1,0:T(8,128)(2,1)S(1)}, bf16[512,512]{1,0:T(8,128)(2,1)}, u32[]{:S(2)}) copy-start(bf16[512,512]{1,0:T(8,128)(2,1)} %constant.10.inv) | copy-start | bytes 1572868
  1.3 11.9 %copy-start.3 = (bf16[512,512]{1,0:T(8,128)(2,1)S(1)}, bf16[512,512]{1,0:T(8,128)(2,1)}, u32[]{:S(2)}) copy-start(bf16[512,512]{1,0:T(8,128)(2,1)} %constant.9.fwd) | copy-start | bytes 1572868
  1.3 11.9 %copy-start.4 = (s32[1,1,2,8]{3,2,1,0:T(2,128)S(1)}, s32[1,1,2,8]{3,2,1,0:T(2,128)}, u32[]{:S(2)}) copy-start(s32[1,1,2,8]{3,2,1,0:T(2,128)} %param.10) | copy-start | bytes 196

commit v2 on v1

--- a/solution.py
+++ b/solution.py
@@ -282,9 +282,13 @@
     direct = DIRECT * side_rows // 4
     return pl.pallas_call(
         halo_kernel,
-        out_shape=(tiled, tiled, jax.ShapeDtypeStruct((probe_size // LANES, LANES), jnp.float32)),
+        out_shape=(
+            tiled,
+            tiled,
+            jax.ShapeDtypeStruct((probe_size // LANES, LANES), jnp.float32),
+        ),
         in_specs=[pl.BlockSpec(memory_space=pltpu.HBM)],
-        out_specs=(vmem, vmem, vmem),
+        out_specs=3 * (vmem,),
         scratch_shapes=[
             pltpu.VMEM(object_field.shape, kind),
             pltpu.SemaphoreType.DMA,
@@ -305,11 +309,11 @@
     )(pltpu.with_memory_space_constraint(object_field, pltpu.HBM))
 
 
-def reduce_kernel(scale, acc_ref, pacc_ref, grad_ref, probe_ref, *scratch):
+def reduce_kernel(scale, acc_ref, pacc_ref, grad_ref, full, *scratch):
     count = len(SIDES)
     sends, landings, rest = scratch[:count], scratch[count : 2 * count], scratch[2 * count :]
-    psend, pair_recv, merged, precv, sums, zbuf, full = rest[:7]
-    side_sems, pair_sems, col_sems, row_sems = rest[7:]
+    psend, pair_recv, merged, precv, sums, zbuf = rest[:6]
+    side_sems, pair_sems, col_sems, row_sems = rest[6:]
     row, col, n_row, n_col = position()
     side_rows, side_cols = grad_ref.shape[1:]
     margin = HALO // LANES
@@ -486,15 +490,6 @@
     for h in range(PARTS):
         for k in range(n_chip):
             forward_copy(h, k, 1 - core).wait_recv()
-    parts, modes, fs, width = probe_ref.shape
-    at = 0
-    for p in range(parts):
-        for m in range(modes):
-            for t in range(width // LANES):
-                probe_ref[p, m, :, t * LANES : (t + 1) * LANES] = full[at : at + fs, :].astype(
-                    jnp.float32
-                )
-                at += fs
     for h in range(PARTS):
         for k in range(1, n_chip):
             scatter_copy(h, k).wait_send()
@@ -511,7 +506,7 @@
             side_copy(index).wait_send()
 
 
-def reduce_call(acc, probe_flat, object_shape, probe_shape, scale):
+def reduce_call(acc, probe_flat, object_shape, scale):
     n_row, n_col = lax.axis_size("row"), lax.axis_size("col")
     _, side_rows, side_cols = object_shape
     inner = side_cols // LANES
@@ -531,7 +526,7 @@
         functools.partial(reduce_kernel, scale),
         out_shape=(
             jax.ShapeDtypeStruct(object_shape, jnp.float32),
-            jax.ShapeDtypeStruct(probe_shape, jnp.float32),
+            jax.ShapeDtypeStruct(probe_flat.shape, jnp.bfloat16),
         ),
         in_specs=[vmem, vmem],
         out_specs=(vmem, vmem),
@@ -544,7 +539,6 @@
             pltpu.VMEM((PARTS, n_chip - 1, piece, LANES), jnp.bfloat16),
             pltpu.VMEM((PARTS, piece, LANES), jnp.float32),
             pltpu.VMEM((PARTS, n_row, piece, LANES), jnp.bfloat16),
-            pltpu.VMEM((total_rows, LANES), jnp.bfloat16),
             pltpu.SemaphoreType.DMA((2, len(SIDES))),
             pltpu.SemaphoreType.DMA((4, PARTS * n_chip)),
             pltpu.SemaphoreType.DMA((4, PARTS * (n_chip - 1))),
@@ -557,6 +551,50 @@
     )(acc, probe_flat)
 
 
+def write_kernel(grad_in, flat_ref, grad_ref, probe_ref, probe_out, sems):
+    grad_copy = pltpu.make_async_copy(grad_in, grad_ref, sems.at[0])
+    grad_copy.start()
+    parts, modes, fs, width = probe_out.shape
+    copies = []
+    at = 0
+    for p in range(parts):
+        for m in range(modes):
+            for t in range(width // LANES):
+                probe_out[p, m, :, t * LANES : (t + 1) * LANES] = flat_ref[at : at + fs, :].astype(
+                    jnp.float32
+                )
+                at += fs
+            copies.append(
+                pltpu.make_async_copy(
+                    probe_out.at[p, m], probe_ref.at[p, m], sems.at[1 + p * modes + m]
+                )
+            )
+            copies[-1].start()
+    for copy in copies:
+        copy.wait()
+    grad_copy.wait()
+
+
+def write_call(grad, probe_flat, probe_shape):
+    vmem = pl.BlockSpec(memory_space=pltpu.VMEM)
+    hbm = pl.BlockSpec(memory_space=pltpu.HBM)
+    return pl.pallas_call(
+        write_kernel,
+        out_shape=(
+            jax.ShapeDtypeStruct(grad.shape, grad.dtype),
+            jax.ShapeDtypeStruct(probe_shape, jnp.float32),
+        ),
+        in_specs=[vmem, vmem],
+        out_specs=(hbm, hbm),
+        scratch_shapes=[
+            pltpu.VMEM(probe_shape, jnp.float32),
+            pltpu.SemaphoreType.DMA((1 + probe_shape[0] * probe_shape[1],)),
+        ],
+        compiler_params=pltpu.CompilerParams(vmem_limit_bytes=8 * 1024 * 1024),
+        name="write",
+    )(grad, probe_flat)
+
+
 def fourier_tables(frame_side):
     indices = np.arange(frame_side)
     product = indices[:, None] * indices[None, :] % frame_side
@@ -582,7 +620,7 @@
     modes = probe_ref.shape[1]
     lane_tiles = fs // LANES
     last_slot = amp_ref.shape[0] - 1
-    live = count_ref[0]
+    live = count_ref[0, 0]
     even, odd = buffers[:4], buffers[4:]
     odd[2][...] = jnp.zeros(odd[2].shape, jnp.float32)
     odd[3][...] = jnp.zeros(odd[3].shape, jnp.float32)
@@ -739,7 +777,7 @@
         ],
         compiler_params=pltpu.CompilerParams(vmem_limit_bytes=26 * 1024 * 1024),
         name="frames",
-    )(live_count.reshape(1), positions, extended, probe_modes, amplitudes, *tables, *zeros)
+    )(live_count, positions, extended, probe_modes, amplitudes, *tables, *zeros)
 
 
 def shards(object_field, probe_modes, measured_amp, scan_positions, frame_counts):
@@ -751,11 +789,12 @@
         probe_modes,
         measured_amp[0, 0],
         scan_positions[0, 0],
-        frame_counts[0, 0],
+        frame_counts,
         fourier_tables(probe_modes.shape[-1]),
     )
     norm_scale = 1.0 / math.sqrt(lax.axis_size("row") * lax.axis_size("col") * slot_count)
-    return reduce_call(acc, probe_flat, object_field.shape, probe_modes.shape, norm_scale)
+    grad, probe_sum = reduce_call(acc, probe_flat, object_field.shape, norm_scale)
+    return write_call(grad, probe_sum, probe_modes.shape)
 
 
 def solution(mesh):

time: 52.3 us -> 51.9 us (level)
  local copies, waits for them, and re-layouts: 2.32 us -> 0.03 us
  Pallas kernels: 48.6 us -> 50.4 us
    unnamed x12 -> x10, local copies, waits for them, and re-layouts: 2.32 us -> 0.03 us
    pallas_call x0 -> x1, Pallas kernels: none -> 1.7 us  [write_call(): pl.pallas_call(write_kernel, out_shape=(jax.ShapeDtypeStruct(grad.shape,...]
where the time goes in v2:
time: 51.9 us; the launch traced here: 51.8 us
  Pallas kernels  50.4 us (97%)
  between operations  1.37 us (3%)
    pallas_call x1, Pallas kernels, reduce_call(): pl.pallas_call(functools.partial(reduce_kernel, scale), out_shape=(jax.Sh...  29.4 us
    pallas_call x1, Pallas kernels, halo_call(): pl.pallas_call(halo_kernel, out_shape=(tiled, tiled, jax.ShapeDtypeStruct...  11.8 us
    pallas_call x1, Pallas kernels, frames_call(): pl.pallas_call(frames_kernel, out_shape=(jax.ShapeDtypeStruct(tiled, jnp....  7.48 us
    pallas_call x1, Pallas kernels, write_call(): pl.pallas_call(write_kernel, out_shape=(jax.ShapeDtypeStruct(grad.shape,...  1.7 us

profile of v2, /device:TPU:0, one launch (start us, length us, event | category | flops | bytes accessed | tf_op | source)
XLA Modules:
  0.0 51.8 jit_solution(13086121087585766504)
XLA Ops:
  1.3 0.0 copy-start
  1.3 0.0 copy-start.1
  1.3 0.0 copy-start.2
  1.3 0.0 copy-start.3
  1.3 0.0 copy-start.4
  1.3 11.8 %halo.1 = (f32[2,7,768,128]{3,2,1,0:T(8,128)S(1)}, f32[2,7,768,128]{3,2,1,0:T(8,128)S(1)}, f32[2048,128]{1,0:T(8,128)S(1)}) custom-call(bf16[2,512,512]{2,1,0:T(8,128)(2,1)} %whole_ref.1), custom_call_target="tpu_custom_call" | custom-call | flops 10000000000 | tf_op jit(solution)/shard_map/halo/pallas_call | solution.py:283
  13.2 0.0 copy-done
  13.2 0.0 copy-done.1
  13.2 0.0 copy-done.2
  13.2 0.0 copy-done.3
  13.2 0.0 copy-done.4
  13.2 7.5 %frames.1 = (f32[2,7,768,128]{3,2,1,0:T(8,128)S(1)}, f32[2048,128]{1,0:T(8,128)S(1)}) custom-call(s32[1,1]{1,0:T(1,128)S(6)} %copy.13.count_ref, s32[2,8]{1,0:T(2,128)S(1)} %bitcast.3, f32[2,7,768,128]{3,2,1,0:T(8,128)S(1)} %get-tuple-element.9.ext_ref, f32[2,2,256,256]{3,2,1,0:T(8,128)S(1)} %copy-done, ...), custom_call_target="tpu_custom_call", output_to_operand_aliasing={{0}: (7, {}), {1}: (8, {})} | custom-call | tf_op jit(solution)/shard_map/frames/pallas_call | solution.py:762
  20.7 29.4 %reduce.1 = (f32[2,512,512]{2,1,0:T(8,128)S(1)}, bf16[2048,128]{1,0:T(8,128)(2,1)S(1)}) custom-call(f32[2,7,768,128]{3,2,1,0:T(8,128)S(1)} %get-tuple-element.12.acc_ref, f32[2048,128]{1,0:T(8,128)S(1)} %get-tuple-element.13.pacc_ref), custom_call_target="tpu_custom_call" | custom-call | tf_op jit(solution)/shard_map/reduce/pallas_call | solution.py:525
  50.1 1.7 %write.1 = (f32[2,512,512]{2,1,0:T(8,128)}, f32[2,2,256,256]{3,2,1,0:T(8,128)}) custom-call(f32[2,512,512]{2,1,0:T(8,128)S(1)} %get-tuple-element.14.grad_in, bf16[2048,128]{1,0:T(8,128)(2,1)S(1)} %get-tuple-element.15.flat_ref), custom_call_target="tpu_custom_call" | custom-call | tf_op jit(solution)/shard_map/write/pallas_call | solution.py:581
Async XLA Ops:
  1.3 11.9 %copy-start = (f32[2,2,256,256]{3,2,1,0:T(8,128)S(1)}, f32[2,2,256,256]{3,2,1,0:T(8,128)}, u32[]{:S(2)}) copy-start(f32[2,2,256,256]{3,2,1,0:T(8,128)} %probe_ref.1) | copy-start | bytes 3145732
  1.3 11.9 %copy-start.1 = (bf16[1,1,8,256,256]{4,3,2,1,0:T(8,128)(2,1)S(1)}, bf16[1,1,8,256,256]{4,3,2,1,0:T(8,128)(2,1)}, u32[]{:S(2)}) copy-start(bf16[1,1,8,256,256]{4,3,2,1,0:T(8,128)(2,1)} %param.9) | copy-start | bytes 3145732
  1.3 11.9 %copy-start.2 = (bf16[512,512]{1,0:T(8,128)(2,1)S(1)}, bf16[512,512]{1,0:T(8,128)(2,1)}, u32[]{:S(2)}) copy-start(bf16[512,512]{1,0:T(8,128)(2,1)} %constant.10.inv) | copy-start | bytes 1572868
  1.3 11.9 %copy-start.3 = (bf16[512,512]{1,0:T(8,128)(2,1)S(1)}, bf16[512,512]{1,0:T(8,128)(2,1)}, u32[]{:S(2)}) copy-start(bf16[512,512]{1,0:T(8,128)(2,1)} %constant.9.fwd) | copy-start | bytes 1572868
  1.3 11.9 %copy-start.4 = (s32[1,1,2,8]{3,2,1,0:T(2,128)S(1)}, s32[1,1,2,8]{3,2,1,0:T(2,128)}, u32[]{:S(2)}) copy-start(s32[1,1,2,8]{3,2,1,0:T(2,128)} %param.10) | copy-start | bytes 196

commit v3 on v2

--- a/solution.py
+++ b/solution.py
@@ -325,23 +325,24 @@
     sibling = (row, 2 * chip + 1 - core)
 
     barrier = pltpu.get_barrier_semaphore()
-    waits = jnp.int32(n_row + n_chip - 1)
+    levels = n_row.bit_length() - 1
+    assert n_row == 2**levels
+    waits = jnp.int32(levels + n_chip)
     pl.semaphore_signal(barrier, inc=1, device_id=sibling, device_id_type=MESH)
     for k in range(1, n_chip):
         peer = (row, 2 * lax.rem(chip + k, n_chip) + core)
         pl.semaphore_signal(barrier, inc=1, device_id=peer, device_id_type=MESH)
-    for k in range(1, n_row):
-        pl.semaphore_signal(
-            barrier, inc=1, device_id=(lax.rem(row + k, n_row), col), device_id_type=MESH
-        )
+    for k in range(levels):
+        size = 2**k
+        peer = (row + size - 2 * size * lax.rem(row // size, 2), col)
+        pl.semaphore_signal(barrier, inc=1, device_id=peer, device_id_type=MESH)
     for side in SIDES:
-        if side[1]:
-
-            @pl.when(exists(side))
-            def _(side=side):
-                pl.semaphore_signal(barrier, inc=1, device_id=at_side(side), device_id_type=MESH)
-
-            waits = waits + exists(side).astype(jnp.int32)
+
+        @pl.when(exists(side))
+        def _(side=side):
+            pl.semaphore_signal(barrier, inc=1, device_id=at_side(side), device_id_type=MESH)
+
+        waits = waits + exists(side).astype(jnp.int32)
 
     def stage_side(index):
         dr, dc = SIDES[index]
@@ -385,10 +386,13 @@
         at = h * (n_chip - 1) + k - 1
         return to_peer(merged.at[h, k - 1], precv.at[h, k - 1], col_sems, 0, at, chip_peer(k))
 
-    def row_copy(h, k, owner):
-        at = h * (n_row - 1) + k - 1
-        peer = (lax.rem(row + k, n_row), col)
-        return to_peer(zbuf.at[h, row], zbuf.at[h, owner], row_sems, 0, at, peer)
+    def row_peer(k):
+        size = 2**k
+        return row + size - 2 * size * lax.rem(row // size, 2)
+
+    def row_copy(h, k):
+        source, landing = zbuf.at[h, 2 * k], zbuf.at[h, 2 * k + 1]
+        return to_peer(source, landing, row_sems, 0, h * levels + k, (row_peer(k), col))
 
     def gather_copy(h, k, owner):
         at = h * (n_chip - 1) + k - 1
@@ -465,20 +469,21 @@
         for k in range(1, n_chip):
             scatter_copy(h, k).wait_recv()
             total = total + precv[h, k - 1].astype(jnp.float32)
-        zbuf[h, row] = total.astype(jnp.bfloat16)
-        for k in range(1, n_row):
-            row_copy(h, k, row).start()
+        zbuf[h, 0] = total.astype(jnp.bfloat16)
+        row_copy(h, 0).start()
+    for k in range(levels):
+        for h in range(PARTS):
+            row_copy(h, k).wait_recv()
+            total = zbuf[h, 2 * k].astype(jnp.float32) + zbuf[h, 2 * k + 1].astype(jnp.float32)
+            if k + 1 < levels:
+                zbuf[h, 2 * k + 2] = total.astype(jnp.bfloat16)
+                row_copy(h, k + 1).start()
+                continue
+            full[rows_of(col, h), :] = (total * scale).astype(jnp.bfloat16)
+            for peer in range(1, n_chip):
+                gather_copy(h, peer, col).start()
+            forward_copy(h, 0, core).start()
     start_sides(corners)
-    for h in range(PARTS):
-        for k in range(1, n_row):
-            row_copy(h, k, lax.rem(row + n_row - k, n_row)).wait_recv()
-        total = zbuf[h, 0].astype(jnp.float32)
-        for k in range(1, n_row):
-            total = total + zbuf[h, k].astype(jnp.float32)
-        full[rows_of(col, h), :] = (total * scale).astype(jnp.bfloat16)
-        for k in range(1, n_chip):
-            gather_copy(h, k, col).start()
-        forward_copy(h, 0, core).start()
     add_sides(over_rows)
     add_sides(over_cols)
     for h in range(PARTS):
@@ -497,8 +502,8 @@
         for k in range(n_chip):
             pair_copy(h, k).wait_send()
             forward_copy(h, k, core).wait_send()
-        for k in range(1, n_row):
-            row_copy(h, k, row).wait_send()
+        for k in range(levels):
+            row_copy(h, k).wait_send()
     for index, side in enumerate(SIDES):
 
         @pl.when(exists(side))
@@ -522,6 +527,7 @@
     total_rows = probe_flat.shape[0]
     piece = total_rows // n_col // PARTS
     n_chip = n_col // 2
+    levels = n_row.bit_length() - 1
     return pl.pallas_call(
         functools.partial(reduce_kernel, scale),
         out_shape=(
@@ -538,11 +544,11 @@
             pltpu.VMEM((PARTS, n_chip - 1, piece, LANES), jnp.bfloat16),
             pltpu.VMEM((PARTS, n_chip - 1, piece, LANES), jnp.bfloat16),
             pltpu.VMEM((PARTS, piece, LANES), jnp.float32),
-            pltpu.VMEM((PARTS, n_row, piece, LANES), jnp.bfloat16),
+            pltpu.VMEM((PARTS, 2 * levels, piece, LANES), jnp.bfloat16),
             pltpu.SemaphoreType.DMA((2, len(SIDES))),
             pltpu.SemaphoreType.DMA((4, PARTS * n_chip)),
             pltpu.SemaphoreType.DMA((4, PARTS * (n_chip - 1))),
-            pltpu.SemaphoreType.DMA((2, PARTS * (n_row - 1))),
+            pltpu.SemaphoreType.DMA((2, PARTS * levels)),
         ],
         compiler_params=pltpu.CompilerParams(
             collective_id=1, has_side_effects=True, vmem_limit_bytes=20 * 1024 * 1024

time: 51.9 us -> 52.3 us (level)
  the two profiles are of different devices: /device:TPU:0 before, /device:TPU:9 now
where the time goes in v3:
time: 52.3 us; the launch traced here: 51.5 us
  Pallas kernels  50.1 us (96%)
  between operations  1.37 us (3%)
    pallas_call x1, Pallas kernels, reduce_call(): pl.pallas_call(functools.partial(reduce_kernel, scale), out_shape=(jax.Sh...  26.1 us
    pallas_call x1, Pallas kernels, halo_call(): pl.pallas_call(halo_kernel, out_shape=(tiled, tiled, jax.ShapeDtypeStruct...  11.6 us
    pallas_call x1, Pallas kernels, frames_call(): pl.pallas_call(frames_kernel, out_shape=(jax.ShapeDtypeStruct(tiled, jnp....  10.7 us
    pallas_call x1, Pallas kernels, write_call(): pl.pallas_call(write_kernel, out_shape=(jax.ShapeDtypeStruct(grad.shape,...  1.7 us

profile of v3, /device:TPU:9, one launch (start us, length us, event | category | flops | bytes accessed | tf_op | source)
XLA Modules:
  0.0 51.5 jit_solution(6721687867275434875)
XLA Ops:
  1.3 0.0 copy-start
  1.3 0.0 copy-start.1
  1.3 0.0 copy-start.2
  1.3 0.0 copy-start.3
  1.3 0.0 copy-start.4
  1.3 11.6 %halo.1 = (f32[2,7,768,128]{3,2,1,0:T(8,128)S(1)}, f32[2,7,768,128]{3,2,1,0:T(8,128)S(1)}, f32[2048,128]{1,0:T(8,128)S(1)}) custom-call(bf16[2,512,512]{2,1,0:T(8,128)(2,1)} %whole_ref.1), custom_call_target="tpu_custom_call" | custom-call | flops 10000000000 | tf_op jit(solution)/shard_map/halo/pallas_call | solution.py:283
  12.9 0.0 copy-done
  13.0 0.0 copy-done.1
  13.0 0.0 copy-done.2
  13.0 0.0 copy-done.3
  13.0 0.0 copy-done.4
  13.0 10.7 %frames.1 = (f32[2,7,768,128]{3,2,1,0:T(8,128)S(1)}, f32[2048,128]{1,0:T(8,128)S(1)}) custom-call(s32[1,1]{1,0:T(1,128)S(6)} %copy.13.count_ref, s32[2,8]{1,0:T(2,128)S(1)} %bitcast.3, f32[2,7,768,128]{3,2,1,0:T(8,128)S(1)} %get-tuple-element.9.ext_ref, f32[2,2,256,256]{3,2,1,0:T(8,128)S(1)} %copy-done, ...), custom_call_target="tpu_custom_call", output_to_operand_aliasing={{0}: (7, {}), {1}: (8, {})} | custom-call | tf_op jit(solution)/shard_map/frames/pallas_call | solution.py:768
  23.7 26.1 %reduce.1 = (f32[2,512,512]{2,1,0:T(8,128)S(1)}, bf16[2048,128]{1,0:T(8,128)(2,1)S(1)}) custom-call(f32[2,7,768,128]{3,2,1,0:T(8,128)S(1)} %get-tuple-element.12.acc_ref, f32[2048,128]{1,0:T(8,128)S(1)} %get-tuple-element.13.pacc_ref), custom_call_target="tpu_custom_call" | custom-call | tf_op jit(solution)/shard_map/reduce/pallas_call | solution.py:531
  49.8 1.7 %write.1 = (f32[2,512,512]{2,1,0:T(8,128)}, f32[2,2,256,256]{3,2,1,0:T(8,128)}) custom-call(f32[2,512,512]{2,1,0:T(8,128)S(1)} %get-tuple-element.14.grad_in, bf16[2048,128]{1,0:T(8,128)(2,1)S(1)} %get-tuple-element.15.flat_ref), custom_call_target="tpu_custom_call" | custom-call | tf_op jit(solution)/shard_map/write/pallas_call | solution.py:587
Async XLA Ops:
  1.3 11.7 %copy-start = (f32[2,2,256,256]{3,2,1,0:T(8,128)S(1)}, f32[2,2,256,256]{3,2,1,0:T(8,128)}, u32[]{:S(2)}) copy-start(f32[2,2,256,256]{3,2,1,0:T(8,128)} %probe_ref.1) | copy-start | bytes 3145732
  1.3 11.7 %copy-start.1 = (bf16[1,1,8,256,256]{4,3,2,1,0:T(8,128)(2,1)S(1)}, bf16[1,1,8,256,256]{4,3,2,1,0:T(8,128)(2,1)}, u32[]{:S(2)}) copy-start(bf16[1,1,8,256,256]{4,3,2,1,0:T(8,128)(2,1)} %param.9) | copy-start | bytes 3145732
  1.3 11.7 %copy-start.2 = (bf16[512,512]{1,0:T(8,128)(2,1)S(1)}, bf16[512,512]{1,0:T(8,128)(2,1)}, u32[]{:S(2)}) copy-start(bf16[512,512]{1,0:T(8,128)(2,1)} %constant.10.inv) | copy-start | bytes 1572868
  1.3 11.7 %copy-start.3 = (bf16[512,512]{1,0:T(8,128)(2,1)S(1)}, bf16[512,512]{1,0:T(8,128)(2,1)}, u32[]{:S(2)}) copy-start(bf16[512,512]{1,0:T(8,128)(2,1)} %constant.9.fwd) | copy-start | bytes 1572868
  1.3 11.7 %copy-start.4 = (s32[1,1,2,8]{3,2,1,0:T(2,128)S(1)}, s32[1,1,2,8]{3,2,1,0:T(2,128)}, u32[]{:S(2)}) copy-start(s32[1,1,2,8]{3,2,1,0:T(2,128)} %param.10) | copy-start | bytes 196

commit v4 on v2

--- a/solution.py
+++ b/solution.py
@@ -70,7 +70,8 @@
     )
 
 
-DIRECT = 1
+DIRECT = 2
+WRITES = 4
 
 
 def halo_kernel(whole_ref, ext_ref, acc_ref, pacc_ref, *scratch):
@@ -552,10 +553,16 @@
 
 
 def write_kernel(grad_in, flat_ref, grad_ref, probe_ref, probe_out, sems):
-    grad_copy = pltpu.make_async_copy(grad_in, grad_ref, sems.at[0])
-    grad_copy.start()
     parts, modes, fs, width = probe_out.shape
+    planes, side_rows, _ = grad_in.shape
+    height = side_rows // WRITES
     copies = []
+    for p in range(planes):
+        for k in range(WRITES):
+            block = (p, slice(k * height, (k + 1) * height))
+            sem = sems.at[parts * modes + p * WRITES + k]
+            copies.append(pltpu.make_async_copy(grad_in.at[block], grad_ref.at[block], sem))
+            copies[-1].start()
     at = 0
     for p in range(parts):
         for m in range(modes):
@@ -566,13 +573,12 @@
                 at += fs
             copies.append(
                 pltpu.make_async_copy(
-                    probe_out.at[p, m], probe_ref.at[p, m], sems.at[1 + p * modes + m]
+                    probe_out.at[p, m], probe_ref.at[p, m], sems.at[p * modes + m]
                 )
             )
             copies[-1].start()
     for copy in copies:
         copy.wait()
-    grad_copy.wait()
 
 
 def write_call(grad, probe_flat, probe_shape):
@@ -588,7 +594,7 @@
         out_specs=(hbm, hbm),
         scratch_shapes=[
             pltpu.VMEM(probe_shape, jnp.float32),
-            pltpu.SemaphoreType.DMA((1 + probe_shape[0] * probe_shape[1],)),
+            pltpu.SemaphoreType.DMA((probe_shape[0] * probe_shape[1] + grad.shape[0] * WRITES,)),
         ],
         compiler_params=pltpu.CompilerParams(vmem_limit_bytes=8 * 1024 * 1024),
         name="write",

time: 51.9 us -> 51.1 us (0.985)
  Pallas kernels: 50.4 us -> 49.7 us
    pallas_call x1, Pallas kernels: 29.4 us -> 22.2 us  [reduce_call(): pl.pallas_call(functools.partial(reduce_kernel, scale), out_shape=(jax.Sh...]
    pallas_call x1, Pallas kernels: 7.48 us -> 13.9 us  [frames_call(): pl.pallas_call(frames_kernel, out_shape=(jax.ShapeDtypeStruct(tiled, jnp....]
where the time goes in v4:
time: 51.1 us
  Pallas kernels  49.7 us (97%)
  between operations  1.37 us (3%)
    pallas_call x1, Pallas kernels, reduce_call(): pl.pallas_call(functools.partial(reduce_kernel, scale), out_shape=(jax.Sh...  22.2 us
    pallas_call x1, Pallas kernels, frames_call(): pl.pallas_call(frames_kernel, out_shape=(jax.ShapeDtypeStruct(tiled, jnp....  13.9 us
    pallas_call x1, Pallas kernels, halo_call(): pl.pallas_call(halo_kernel, out_shape=(tiled, tiled, jax.ShapeDtypeStruct...  11.8 us
    pallas_call x1, Pallas kernels, write_call(): pl.pallas_call(write_kernel, out_shape=(jax.ShapeDtypeStruct(grad.shape,...  1.76 us

profile of v4, /device:TPU:0, one launch (start us, length us, event | category | flops | bytes accessed | tf_op | source)
XLA Modules:
  0.0 51.1 jit_solution(10887858377091859588)
XLA Ops:
  1.3 0.0 copy-start
  1.3 0.0 copy-start.1
  1.3 0.0 copy-start.2
  1.3 0.0 copy-start.3
  1.3 0.0 copy-start.4
  1.3 11.8 %halo.1 = (f32[2,7,768,128]{3,2,1,0:T(8,128)S(1)}, f32[2,7,768,128]{3,2,1,0:T(8,128)S(1)}, f32[2048,128]{1,0:T(8,128)S(1)}) custom-call(bf16[2,512,512]{2,1,0:T(8,128)(2,1)} %whole_ref.1), custom_call_target="tpu_custom_call" | custom-call | flops 10000000000 | tf_op jit(solution)/shard_map/halo/pallas_call | solution.py:284
  13.2 0.0 copy-done
  13.2 0.0 copy-done.1
  13.2 0.0 copy-done.2
  13.2 0.0 copy-done.3
  13.2 0.0 copy-done.4
  13.2 13.9 %frames.1 = (f32[2,7,768,128]{3,2,1,0:T(8,128)S(1)}, f32[2048,128]{1,0:T(8,128)S(1)}) custom-call(s32[1,1]{1,0:T(1,128)S(6)} %copy.13.count_ref, s32[2,8]{1,0:T(2,128)S(1)} %bitcast.3, f32[2,7,768,128]{3,2,1,0:T(8,128)S(1)} %get-tuple-element.9.ext_ref, f32[2,2,256,256]{3,2,1,0:T(8,128)S(1)} %copy-done, ...), custom_call_target="tpu_custom_call", output_to_operand_aliasing={{0}: (7, {}), {1}: (8, {})} | custom-call | tf_op jit(solution)/shard_map/frames/pallas_call | solution.py:768
  27.1 22.2 %reduce.1 = (f32[2,512,512]{2,1,0:T(8,128)S(1)}, bf16[2048,128]{1,0:T(8,128)(2,1)S(1)}) custom-call(f32[2,7,768,128]{3,2,1,0:T(8,128)S(1)} %get-tuple-element.12.acc_ref, f32[2048,128]{1,0:T(8,128)S(1)} %get-tuple-element.13.pacc_ref), custom_call_target="tpu_custom_call" | custom-call | tf_op jit(solution)/shard_map/reduce/pallas_call | solution.py:526
  49.3 1.8 %write.1 = (f32[2,512,512]{2,1,0:T(8,128)}, f32[2,2,256,256]{3,2,1,0:T(8,128)}) custom-call(f32[2,512,512]{2,1,0:T(8,128)S(1)} %get-tuple-element.14.grad_in, bf16[2048,128]{1,0:T(8,128)(2,1)S(1)} %get-tuple-element.15.flat_ref), custom_call_target="tpu_custom_call" | custom-call | tf_op jit(solution)/shard_map/write/pallas_call | solution.py:587
Async XLA Ops:
  1.3 11.9 %copy-start = (f32[2,2,256,256]{3,2,1,0:T(8,128)S(1)}, f32[2,2,256,256]{3,2,1,0:T(8,128)}, u32[]{:S(2)}) copy-start(f32[2,2,256,256]{3,2,1,0:T(8,128)} %probe_ref.1) | copy-start | bytes 3145732
  1.3 11.9 %copy-start.1 = (bf16[1,1,8,256,256]{4,3,2,1,0:T(8,128)(2,1)S(1)}, bf16[1,1,8,256,256]{4,3,2,1,0:T(8,128)(2,1)}, u32[]{:S(2)}) copy-start(bf16[1,1,8,256,256]{4,3,2,1,0:T(8,128)(2,1)} %param.9) | copy-start | bytes 3145732
  1.3 11.9 %copy-start.2 = (bf16[512,512]{1,0:T(8,128)(2,1)S(1)}, bf16[512,512]{1,0:T(8,128)(2,1)}, u32[]{:S(2)}) copy-start(bf16[512,512]{1,0:T(8,128)(2,1)} %constant.10.inv) | copy-start | bytes 1572868
  1.3 11.9 %copy-start.3 = (bf16[512,512]{1,0:T(8,128)(2,1)S(1)}, bf16[512,512]{1,0:T(8,128)(2,1)}, u32[]{:S(2)}) copy-start(bf16[512,512]{1,0:T(8,128)(2,1)} %constant.9.fwd) | copy-start | bytes 1572868
  1.3 11.9 %copy-start.4 = (s32[1,1,2,8]{3,2,1,0:T(2,128)S(1)}, s32[1,1,2,8]{3,2,1,0:T(2,128)}, u32[]{:S(2)}) copy-start(s32[1,1,2,8]{3,2,1,0:T(2,128)} %param.10) | copy-start | bytes 196

commit v5 on v2

--- a/solution.py
+++ b/solution.py
@@ -70,7 +70,7 @@
     )
 
 
-DIRECT = 1
+DIRECT = 2
 
 
 def halo_kernel(whole_ref, ext_ref, acc_ref, pacc_ref, *scratch):
@@ -309,11 +309,11 @@
     )(pltpu.with_memory_space_constraint(object_field, pltpu.HBM))
 
 
-def reduce_kernel(scale, acc_ref, pacc_ref, grad_ref, full, *scratch):
+def reduce_kernel(scale, acc_ref, pacc_ref, grad_ref, flat_ref, *scratch):
     count = len(SIDES)
     sends, landings, rest = scratch[:count], scratch[count : 2 * count], scratch[2 * count :]
-    psend, pair_recv, merged, precv, sums, zbuf = rest[:6]
-    side_sems, pair_sems, col_sems, row_sems = rest[6:]
+    psend, pair_recv, merged, precv, sums, zbuf, full = rest[:7]
+    side_sems, strip_sems, pair_sems, col_sems, row_sems = rest[7:]
     row, col, n_row, n_col = position()
     side_rows, side_cols = grad_ref.shape[1:]
     margin = HALO // LANES
@@ -335,7 +335,7 @@
             barrier, inc=1, device_id=(lax.rem(row + k, n_row), col), device_id_type=MESH
         )
     for side in SIDES:
-        if side[1]:
+        if side[0] == 0:
 
             @pl.when(exists(side))
             def _(side=side):
@@ -401,9 +401,70 @@
         return to_peer(source, landing, pair_sems, 2, h * n_chip + k, sibling)
 
     def side_copy(index):
+        side = (0, SIDES[index][1])
         return to_side(
-            SIDES[index], index, sends[index], landings[index], side_sems.at[0], side_sems.at[1]
-        )
+            side, index, sends[index], landings[index], side_sems.at[0], side_sems.at[1]
+        )
+
+    strips = [index for index, side in enumerate(SIDES) if side[1] == 0]
+    pieces = (slice(margin, inner - margin), slice(0, margin), slice(inner - margin, inner))
+
+    def strip_copy(r, p):
+        index = strips[r]
+        source, landing = sends[index].at[:, pieces[p]], landings[index].at[:, pieces[p]]
+        return to_peer(source, landing, strip_sems, 0, 3 * r + p, at_side(SIDES[index]))
+
+    def start_middles():
+        for r, index in enumerate(strips):
+            dr = SIDES[index][0]
+            for k in range(margin, inner - margin):
+                sends[index][:, k] = acc_ref[:, margin + k, part(dr, HALO, side_rows), :].astype(
+                    jnp.bfloat16
+                )
+
+            @pl.when(exists(SIDES[index]))
+            def _(r=r):
+                strip_copy(r, 0).start()
+
+    def start_edges():
+        for r, index in enumerate(strips):
+            dr = SIDES[index][0]
+            for p, dc in ((1, -1), (2, 1)):
+                corner = SIDES.index((dr, -dc))
+                tiles = range(inner)[pieces[p]]
+                rows = part(dr, HALO, side_rows)
+
+                @pl.when(exists((dr, dc)))
+                def _(index=index, corner=corner, tiles=tiles, rows=rows):
+                    side_copy(corner).wait_recv()
+                    for k, t in enumerate(tiles):
+                        own = acc_ref[:, margin + t, rows, :]
+                        sends[index][:, t] = (
+                            own + landings[corner][:, k].astype(jnp.float32)
+                        ).astype(jnp.bfloat16)
+
+                @pl.when(jnp.logical_and(exists((dr, 0)), jnp.logical_not(exists((0, dc)))))
+                def _(index=index, tiles=tiles, rows=rows):
+                    for t in tiles:
+                        sends[index][:, t] = acc_ref[:, margin + t, rows, :].astype(jnp.bfloat16)
+
+                @pl.when(exists((dr, 0)))
+                def _(r=r, p=p):
+                    strip_copy(r, p).start()
+
+    def add_rows():
+        for r, index in enumerate(strips):
+            dr = -SIDES[index][0]
+            rows = edge(dr, HALO, side_rows)
+
+            @pl.when(exists((dr, 0)))
+            def _(r=r, index=index, rows=rows):
+                for p in range(3):
+                    strip_copy(r, p).wait_recv()
+                for t in range(inner):
+                    grad_ref[:, rows, t * LANES : (t + 1) * LANES] += landings[index][
+                        :, t
+                    ].astype(jnp.float32)
 
     def start_sides(chosen):
         for index, side in enumerate(SIDES):
@@ -429,21 +490,20 @@
                         :, k
                     ].astype(jnp.float32)
 
-    over_rows = lambda side: side[1] == 0
     over_cols = lambda side: side[0] == 0
     corners = lambda side: side[0] != 0 and side[1] != 0
     order = list(range(1, n_chip)) + [0]
     for h in range(PARTS):
         for k in order:
             psend[h, k] = pacc_ref[rows_of(2 * chip_at(k) + 1 - core, h), :].astype(jnp.bfloat16)
-    stage_sides(over_rows)
+    stage_sides(corners)
     pl.semaphore_wait(barrier, waits)
     for h in range(PARTS):
         for k in order:
             pair_copy(h, k).start()
-    start_sides(over_rows)
+    start_sides(corners)
+    start_middles()
     stage_sides(over_cols)
-    stage_sides(corners)
 
     def merge(h, k):
         pair_copy(h, k).wait_recv()
@@ -455,6 +515,7 @@
             merged[h, k - 1] = merge(h, k).astype(jnp.bfloat16)
             scatter_copy(h, k).start()
         sums[h] = merge(h, 0)
+    start_edges()
     start_sides(over_cols)
     for t in range(inner):
         grad_ref[:, :, t * LANES : (t + 1) * LANES] = acc_ref[
@@ -468,7 +529,6 @@
         zbuf[h, row] = total.astype(jnp.bfloat16)
         for k in range(1, n_row):
             row_copy(h, k, row).start()
-    start_sides(corners)
     for h in range(PARTS):
         for k in range(1, n_row):
             row_copy(h, k, lax.rem(row + n_row - k, n_row)).wait_recv()
@@ -479,17 +539,23 @@
         for k in range(1, n_chip):
             gather_copy(h, k, col).start()
         forward_copy(h, 0, core).start()
-    add_sides(over_rows)
+
+    def unpack(h, k, side):
+        rows = rows_of(2 * chip_from(k) + side, h)
+        flat_ref[rows, :] = full[rows, :].astype(jnp.float32)
+
+    add_rows()
     add_sides(over_cols)
     for h in range(PARTS):
+        unpack(h, 0, core)
         for k in range(1, n_chip):
             gather_copy(h, k, 2 * chip_from(k) + core).wait_recv()
             forward_copy(h, k, core).start()
-    add_sides(corners)
-
+            unpack(h, k, core)
     for h in range(PARTS):
         for k in range(n_chip):
             forward_copy(h, k, 1 - core).wait_recv()
+            unpack(h, k, 1 - core)
     for h in range(PARTS):
         for k in range(1, n_chip):
             scatter_copy(h, k).wait_send()
@@ -503,7 +569,11 @@
 
         @pl.when(exists(side))
         def _(index=index):
-            side_copy(index).wait_send()
+            if index in strips:
+                for p in range(3):
+                    strip_copy(strips.index(index), p).wait_send()
+            else:
+                side_copy(index).wait_send()
 
 
 def reduce_call(acc, probe_flat, object_shape, scale):
@@ -526,7 +596,7 @@
         functools.partial(reduce_kernel, scale),
         out_shape=(
             jax.ShapeDtypeStruct(object_shape, jnp.float32),
-            jax.ShapeDtypeStruct(probe_flat.shape, jnp.bfloat16),
+            jax.ShapeDtypeStruct(probe_flat.shape, jnp.float32),
         ),
         in_specs=[vmem, vmem],
         out_specs=(vmem, vmem),
@@ -539,7 +609,9 @@
             pltpu.VMEM((PARTS, n_chip - 1, piece, LANES), jnp.bfloat16),
             pltpu.VMEM((PARTS, piece, LANES), jnp.float32),
             pltpu.VMEM((PARTS, n_row, piece, LANES), jnp.bfloat16),
+            pltpu.VMEM((total_rows, LANES), jnp.bfloat16),
             pltpu.SemaphoreType.DMA((2, len(SIDES))),
+            pltpu.SemaphoreType.DMA((2, 6)),
             pltpu.SemaphoreType.DMA((4, PARTS * n_chip)),
             pltpu.SemaphoreType.DMA((4, PARTS * (n_chip - 1))),
             pltpu.SemaphoreType.DMA((2, PARTS * (n_row - 1))),
@@ -551,33 +623,28 @@
     )(acc, probe_flat)
 
 
-def write_kernel(grad_in, flat_ref, grad_ref, probe_ref, probe_out, sems):
-    grad_copy = pltpu.make_async_copy(grad_in, grad_ref, sems.at[0])
-    grad_copy.start()
-    parts, modes, fs, width = probe_out.shape
+def write_kernel(grad_in, flat_ref, grad_ref, probe_ref, sems):
+    parts, modes, fs, width = probe_ref.shape
     copies = []
-    at = 0
     for p in range(parts):
         for m in range(modes):
             for t in range(width // LANES):
-                probe_out[p, m, :, t * LANES : (t + 1) * LANES] = flat_ref[at : at + fs, :].astype(
-                    jnp.float32
-                )
-                at += fs
-            copies.append(
-                pltpu.make_async_copy(
-                    probe_out.at[p, m], probe_ref.at[p, m], sems.at[1 + p * modes + m]
-                )
-            )
-            copies[-1].start()
+                at = len(copies) * fs
+                target = probe_ref.at[p, m, :, t * LANES : (t + 1) * LANES]
+                sem = sems.at[len(copies)]
+                copies.append(pltpu.make_async_copy(flat_ref.at[at : at + fs, :], target, sem))
+    for p in range(grad_in.shape[0]):
+        copies.append(pltpu.make_async_copy(grad_in.at[p], grad_ref.at[p], sems.at[len(copies)]))
+    for copy in copies:
+        copy.start()
     for copy in copies:
         copy.wait()
-    grad_copy.wait()
 
 
 def write_call(grad, probe_flat, probe_shape):
     vmem = pl.BlockSpec(memory_space=pltpu.VMEM)
     hbm = pl.BlockSpec(memory_space=pltpu.HBM)
+    count = probe_flat.shape[0] // probe_shape[2] + grad.shape[0]
     return pl.pallas_call(
         write_kernel,
         out_shape=(
@@ -586,10 +653,7 @@
         ),
         in_specs=[vmem, vmem],
         out_specs=(hbm, hbm),
-        scratch_shapes=[
-            pltpu.VMEM(probe_shape, jnp.float32),
-            pltpu.SemaphoreType.DMA((1 + probe_shape[0] * probe_shape[1],)),
-        ],
+        scratch_shapes=[pltpu.SemaphoreType.DMA((count,))],
         compiler_params=pltpu.CompilerParams(vmem_limit_bytes=8 * 1024 * 1024),
         name="write",
     )(grad, probe_flat)

time: 51.9 us -> 51.2 us (0.987)
  Pallas kernels: 50.4 us -> 49.3 us
    pallas_call x1, Pallas kernels: 29.4 us -> 28.3 us  [reduce_call(): pl.pallas_call(functools.partial(reduce_kernel, scale), out_shape=(jax.Sh...]
where the time goes in v5:
time: 51.2 us; the launch traced here: 50.7 us
  Pallas kernels  49.3 us (96%)
  between operations  1.38 us (3%)
    pallas_call x1, Pallas kernels, reduce_call(): pl.pallas_call(functools.partial(reduce_kernel, scale), out_shape=(jax.Sh...  28.3 us
    pallas_call x1, Pallas kernels, halo_call(): pl.pallas_call(halo_kernel, out_shape=(tiled, tiled, jax.ShapeDtypeStruct...  11.8 us
    pallas_call x1, Pallas kernels, frames_call(): pl.pallas_call(frames_kernel, out_shape=(jax.ShapeDtypeStruct(tiled, jnp....  7.46 us
    pallas_call x1, Pallas kernels, write_call(): pl.pallas_call(write_kernel, out_shape=(jax.ShapeDtypeStruct(grad.shape,...  1.75 us

profile of v5, /device:TPU:0, one launch (start us, length us, event | category | flops | bytes accessed | tf_op | source)
XLA Modules:
  0.0 50.7 jit_solution(14675873094285278454)
XLA Ops:
  1.3 0.0 copy-start
  1.3 0.0 copy-start.1
  1.3 0.0 copy-start.2
  1.3 0.0 copy-start.3
  1.3 0.0 copy-start.4
  1.3 11.8 %halo.1 = (f32[2,7,768,128]{3,2,1,0:T(8,128)S(1)}, f32[2,7,768,128]{3,2,1,0:T(8,128)S(1)}, f32[2048,128]{1,0:T(8,128)S(1)}) custom-call(bf16[2,512,512]{2,1,0:T(8,128)(2,1)} %whole_ref.1), custom_call_target="tpu_custom_call" | custom-call | flops 10000000000 | tf_op jit(solution)/shard_map/halo/pallas_call | solution.py:283
  13.2 0.0 copy-done
  13.2 0.0 copy-done.1
  13.2 0.0 copy-done.2
  13.2 0.0 copy-done.3
  13.2 0.0 copy-done.4
  13.2 7.5 %frames.1 = (f32[2,7,768,128]{3,2,1,0:T(8,128)S(1)}, f32[2048,128]{1,0:T(8,128)S(1)}) custom-call(s32[1,1]{1,0:T(1,128)S(6)} %copy.13.count_ref, s32[2,8]{1,0:T(2,128)S(1)} %bitcast.3, f32[2,7,768,128]{3,2,1,0:T(8,128)S(1)} %get-tuple-element.9.ext_ref, f32[2,2,256,256]{3,2,1,0:T(8,128)S(1)} %copy-done, ...), custom_call_target="tpu_custom_call", output_to_operand_aliasing={{0}: (7, {}), {1}: (8, {})} | custom-call | tf_op jit(solution)/shard_map/frames/pallas_call | solution.py:826
  20.7 28.3 %reduce.1 = (f32[2,512,512]{2,1,0:T(8,128)S(1)}, f32[2048,128]{1,0:T(8,128)S(1)}) custom-call(f32[2,7,768,128]{3,2,1,0:T(8,128)S(1)} %get-tuple-element.12.acc_ref, f32[2048,128]{1,0:T(8,128)S(1)} %get-tuple-element.13.pacc_ref), custom_call_target="tpu_custom_call" | custom-call | tf_op jit(solution)/shard_map/reduce/pallas_call | solution.py:595
  49.0 1.7 %write.1 = (f32[2,512,512]{2,1,0:T(8,128)}, f32[2,2,256,256]{3,2,1,0:T(8,128)}) custom-call(f32[2,512,512]{2,1,0:T(8,128)S(1)} %get-tuple-element.14.grad_in, f32[2048,128]{1,0:T(8,128)S(1)} %get-tuple-element.15.flat_ref), custom_call_target="tpu_custom_call" | custom-call | tf_op jit(solution)/shard_map/write/pallas_call | solution.py:648
Async XLA Ops:
  1.3 11.9 %copy-start = (f32[2,2,256,256]{3,2,1,0:T(8,128)S(1)}, f32[2,2,256,256]{3,2,1,0:T(8,128)}, u32[]{:S(2)}) copy-start(f32[2,2,256,256]{3,2,1,0:T(8,128)} %probe_ref.1) | copy-start | bytes 3145732
  1.3 11.9 %copy-start.1 = (bf16[1,1,8,256,256]{4,3,2,1,0:T(8,128)(2,1)S(1)}, bf16[1,1,8,256,256]{4,3,2,1,0:T(8,128)(2,1)}, u32[]{:S(2)}) copy-start(bf16[1,1,8,256,256]{4,3,2,1,0:T(8,128)(2,1)} %param.9) | copy-start | bytes 3145732
  1.3 11.9 %copy-start.2 = (bf16[512,512]{1,0:T(8,128)(2,1)S(1)}, bf16[512,512]{1,0:T(8,128)(2,1)}, u32[]{:S(2)}) copy-start(bf16[512,512]{1,0:T(8,128)(2,1)} %constant.10.inv) | copy-start | bytes 1572868
  1.3 11.9 %copy-start.3 = (bf16[512,512]{1,0:T(8,128)(2,1)S(1)}, bf16[512,512]{1,0:T(8,128)(2,1)}, u32[]{:S(2)}) copy-start(bf16[512,512]{1,0:T(8,128)(2,1)} %constant.9.fwd) | copy-start | bytes 1572868
  1.3 11.9 %copy-start.4 = (s32[1,1,2,8]{3,2,1,0:T(2,128)S(1)}, s32[1,1,2,8]{3,2,1,0:T(2,128)}, u32[]{:S(2)}) copy-start(s32[1,1,2,8]{3,2,1,0:T(2,128)} %param.10) | copy-start | bytes 196

commit v6 on v5

--- a/solution.py
+++ b/solution.py
@@ -501,7 +501,6 @@
     for h in range(PARTS):
         for k in order:
             pair_copy(h, k).start()
-    start_sides(corners)
     start_middles()
     stage_sides(over_cols)
 
@@ -515,7 +514,7 @@
             merged[h, k - 1] = merge(h, k).astype(jnp.bfloat16)
             scatter_copy(h, k).start()
         sums[h] = merge(h, 0)
-    start_edges()
+    start_sides(corners)
     start_sides(over_cols)
     for t in range(inner):
         grad_ref[:, :, t * LANES : (t + 1) * LANES] = acc_ref[
@@ -529,6 +528,7 @@
         zbuf[h, row] = total.astype(jnp.bfloat16)
         for k in range(1, n_row):
             row_copy(h, k, row).start()
+    start_edges()
     for h in range(PARTS):
         for k in range(1, n_row):
             row_copy(h, k, lax.rem(row + n_row - k, n_row)).wait_recv()
@@ -544,14 +544,14 @@
         rows = rows_of(2 * chip_from(k) + side, h)
         flat_ref[rows, :] = full[rows, :].astype(jnp.float32)
 
-    add_rows()
-    add_sides(over_cols)
     for h in range(PARTS):
         unpack(h, 0, core)
         for k in range(1, n_chip):
             gather_copy(h, k, 2 * chip_from(k) + core).wait_recv()
             forward_copy(h, k, core).start()
             unpack(h, k, core)
+    add_rows()
+    add_sides(over_cols)
     for h in range(PARTS):
         for k in range(n_chip):
             forward_copy(h, k, 1 - core).wait_recv()

time: 51.2 us -> 49.3 us (0.963); the launches traced: 50.7 us -> 49.9 us
  Pallas kernels: 49.3 us -> 48.5 us
    pallas_call x1, Pallas kernels: 28.3 us -> 24.2 us  [reduce_call(): pl.pallas_call(functools.partial(reduce_kernel, scale), out_shape=(jax.Sh...]
    pallas_call x1, Pallas kernels: 7.46 us -> 10.7 us  [frames_call(): pl.pallas_call(frames_kernel, out_shape=(jax.ShapeDtypeStruct(tiled, jnp....]
where the time goes in v6:
time: 49.3 us; the launch traced here: 49.9 us
  Pallas kernels  48.5 us (98%)
  between operations  1.37 us (3%)
    pallas_call x1, Pallas kernels, reduce_call(): pl.pallas_call(functools.partial(reduce_kernel, scale), out_shape=(jax.Sh...  24.2 us
    pallas_call x1, Pallas kernels, halo_call(): pl.pallas_call(halo_kernel, out_shape=(tiled, tiled, jax.ShapeDtypeStruct...  11.8 us
    pallas_call x1, Pallas kernels, frames_call(): pl.pallas_call(frames_kernel, out_shape=(jax.ShapeDtypeStruct(tiled, jnp....  10.7 us
    pallas_call x1, Pallas kernels, write_call(): pl.pallas_call(write_kernel, out_shape=(jax.ShapeDtypeStruct(grad.shape,...  1.75 us

profile of v6, /device:TPU:0, one launch (start us, length us, event | category | flops | bytes accessed | tf_op | source)
XLA Modules:
  0.0 49.9 jit_solution(12084006923942424596)
XLA Ops:
  1.3 0.0 copy-start
  1.3 0.0 copy-start.1
  1.3 0.0 copy-start.2
  1.3 0.0 copy-start.3
  1.3 0.0 copy-start.4
  1.3 11.8 %halo.1 = (f32[2,7,768,128]{3,2,1,0:T(8,128)S(1)}, f32[2,7,768,128]{3,2,1,0:T(8,128)S(1)}, f32[2048,128]{1,0:T(8,128)S(1)}) custom-call(bf16[2,512,512]{2,1,0:T(8,128)(2,1)} %whole_ref.1), custom_call_target="tpu_custom_call" | custom-call | flops 10000000000 | tf_op jit(solution)/shard_map/halo/pallas_call | solution.py:283
  13.2 0.0 copy-done
  13.2 0.0 copy-done.1
  13.2 0.0 copy-done.2
  13.2 0.0 copy-done.3
  13.2 0.0 copy-done.4
  13.2 10.7 %frames.1 = (f32[2,7,768,128]{3,2,1,0:T(8,128)S(1)}, f32[2048,128]{1,0:T(8,128)S(1)}) custom-call(s32[1,1]{1,0:T(1,128)S(6)} %copy.13.count_ref, s32[2,8]{1,0:T(2,128)S(1)} %bitcast.3, f32[2,7,768,128]{3,2,1,0:T(8,128)S(1)} %get-tuple-element.9.ext_ref, f32[2,2,256,256]{3,2,1,0:T(8,128)S(1)} %copy-done, ...), custom_call_target="tpu_custom_call", output_to_operand_aliasing={{0}: (7, {}), {1}: (8, {})} | custom-call | tf_op jit(solution)/shard_map/frames/pallas_call | solution.py:826
  23.9 24.2 %reduce.1 = (f32[2,512,512]{2,1,0:T(8,128)S(1)}, f32[2048,128]{1,0:T(8,128)S(1)}) custom-call(f32[2,7,768,128]{3,2,1,0:T(8,128)S(1)} %get-tuple-element.12.acc_ref, f32[2048,128]{1,0:T(8,128)S(1)} %get-tuple-element.13.pacc_ref), custom_call_target="tpu_custom_call" | custom-call | tf_op jit(solution)/shard_map/reduce/pallas_call | solution.py:595
  48.1 1.7 %write.1 = (f32[2,512,512]{2,1,0:T(8,128)}, f32[2,2,256,256]{3,2,1,0:T(8,128)}) custom-call(f32[2,512,512]{2,1,0:T(8,128)S(1)} %get-tuple-element.14.grad_in, f32[2048,128]{1,0:T(8,128)S(1)} %get-tuple-element.15.flat_ref), custom_call_target="tpu_custom_call" | custom-call | tf_op jit(solution)/shard_map/write/pallas_call | solution.py:648
Async XLA Ops:
  1.3 11.9 %copy-start = (f32[2,2,256,256]{3,2,1,0:T(8,128)S(1)}, f32[2,2,256,256]{3,2,1,0:T(8,128)}, u32[]{:S(2)}) copy-start(f32[2,2,256,256]{3,2,1,0:T(8,128)} %probe_ref.1) | copy-start | bytes 3145732
  1.3 11.9 %copy-start.1 = (bf16[1,1,8,256,256]{4,3,2,1,0:T(8,128)(2,1)S(1)}, bf16[1,1,8,256,256]{4,3,2,1,0:T(8,128)(2,1)}, u32[]{:S(2)}) copy-start(bf16[1,1,8,256,256]{4,3,2,1,0:T(8,128)(2,1)} %param.9) | copy-start | bytes 3145732
  1.3 11.9 %copy-start.2 = (bf16[512,512]{1,0:T(8,128)(2,1)S(1)}, bf16[512,512]{1,0:T(8,128)(2,1)}, u32[]{:S(2)}) copy-start(bf16[512,512]{1,0:T(8,128)(2,1)} %constant.10.inv) | copy-start | bytes 1572868
  1.3 11.9 %copy-start.3 = (bf16[512,512]{1,0:T(8,128)(2,1)S(1)}, bf16[512,512]{1,0:T(8,128)(2,1)}, u32[]{:S(2)}) copy-start(bf16[512,512]{1,0:T(8,128)(2,1)} %constant.9.fwd) | copy-start | bytes 1572868
  1.3 11.9 %copy-start.4 = (s32[1,1,2,8]{3,2,1,0:T(2,128)S(1)}, s32[1,1,2,8]{3,2,1,0:T(2,128)}, u32[]{:S(2)}) copy-start(s32[1,1,2,8]{3,2,1,0:T(2,128)} %param.10) | copy-start | bytes 196

commit v7 on v6

--- a/solution.py
+++ b/solution.py
@@ -669,7 +669,7 @@
     return tuple(jnp.asarray(table.astype(np.float32)).astype(jnp.bfloat16) for table in tables)
 
 
-CHUNK = 32
+CHUNK = 16
 
 
 def dot32(left, right):

time: 49.3 us -> 49.6 us (level)
    pallas_call x1, Pallas kernels: 24.2 us -> 20.9 us  [reduce_call(): pl.pallas_call(functools.partial(reduce_kernel, scale), out_shape=(jax.Sh...]
    pallas_call x1, Pallas kernels: 10.7 us -> 13.9 us  [frames_call(): pl.pallas_call(frames_kernel, out_shape=(jax.ShapeDtypeStruct(tiled, jnp....]
where the time goes in v7:
time: 49.6 us; the launch traced here: 49.8 us
  Pallas kernels  48.4 us (98%)
  between operations  1.38 us (3%)
    pallas_call x1, Pallas kernels, reduce_call(): pl.pallas_call(functools.partial(reduce_kernel, scale), out_shape=(jax.Sh...  20.9 us
    pallas_call x1, Pallas kernels, frames_call(): pl.pallas_call(frames_kernel, out_shape=(jax.ShapeDtypeStruct(tiled, jnp....  13.9 us
    pallas_call x1, Pallas kernels, halo_call(): pl.pallas_call(halo_kernel, out_shape=(tiled, tiled, jax.ShapeDtypeStruct...  11.8 us
    pallas_call x1, Pallas kernels, write_call(): pl.pallas_call(write_kernel, out_shape=(jax.ShapeDtypeStruct(grad.shape,...  1.75 us

profile of v7, /device:TPU:0, one launch (start us, length us, event | category | flops | bytes accessed | tf_op | source)
XLA Modules:
  0.0 49.8 jit_solution(7464618501294410960)
XLA Ops:
  1.3 0.0 copy-start
  1.3 0.0 copy-start.1
  1.3 0.0 copy-start.2
  1.3 0.0 copy-start.3
  1.3 0.0 copy-start.4
  1.3 11.8 %halo.1 = (f32[2,7,768,128]{3,2,1,0:T(8,128)S(1)}, f32[2,7,768,128]{3,2,1,0:T(8,128)S(1)}, f32[2048,128]{1,0:T(8,128)S(1)}) custom-call(bf16[2,512,512]{2,1,0:T(8,128)(2,1)} %whole_ref.1), custom_call_target="tpu_custom_call" | custom-call | flops 10000000000 | tf_op jit(solution)/shard_map/halo/pallas_call | solution.py:283
  13.2 0.0 copy-done
  13.2 0.0 copy-done.1
  13.2 0.0 copy-done.2
  13.2 0.0 copy-done.3
  13.2 0.0 copy-done.4
  13.2 13.9 %frames.1 = (f32[2,7,768,128]{3,2,1,0:T(8,128)S(1)}, f32[2048,128]{1,0:T(8,128)S(1)}) custom-call(s32[1,1]{1,0:T(1,128)S(6)} %copy.13.count_ref, s32[2,8]{1,0:T(2,128)S(1)} %bitcast.3, f32[2,7,768,128]{3,2,1,0:T(8,128)S(1)} %get-tuple-element.9.ext_ref, f32[2,2,256,256]{3,2,1,0:T(8,128)S(1)} %copy-done, ...), custom_call_target="tpu_custom_call", output_to_operand_aliasing={{0}: (7, {}), {1}: (8, {})} | custom-call | tf_op jit(solution)/shard_map/frames/pallas_call | solution.py:826
  27.1 20.9 %reduce.1 = (f32[2,512,512]{2,1,0:T(8,128)S(1)}, f32[2048,128]{1,0:T(8,128)S(1)}) custom-call(f32[2,7,768,128]{3,2,1,0:T(8,128)S(1)} %get-tuple-element.12.acc_ref, f32[2048,128]{1,0:T(8,128)S(1)} %get-tuple-element.13.pacc_ref), custom_call_target="tpu_custom_call" | custom-call | tf_op jit(solution)/shard_map/reduce/pallas_call | solution.py:595
  48.0 1.7 %write.1 = (f32[2,512,512]{2,1,0:T(8,128)}, f32[2,2,256,256]{3,2,1,0:T(8,128)}) custom-call(f32[2,512,512]{2,1,0:T(8,128)S(1)} %get-tuple-element.14.grad_in, f32[2048,128]{1,0:T(8,128)S(1)} %get-tuple-element.15.flat_ref), custom_call_target="tpu_custom_call" | custom-call | tf_op jit(solution)/shard_map/write/pallas_call | solution.py:648
Async XLA Ops:
  1.3 11.9 %copy-start = (f32[2,2,256,256]{3,2,1,0:T(8,128)S(1)}, f32[2,2,256,256]{3,2,1,0:T(8,128)}, u32[]{:S(2)}) copy-start(f32[2,2,256,256]{3,2,1,0:T(8,128)} %probe_ref.1) | copy-start | bytes 3145732
  1.3 11.9 %copy-start.1 = (bf16[1,1,8,256,256]{4,3,2,1,0:T(8,128)(2,1)S(1)}, bf16[1,1,8,256,256]{4,3,2,1,0:T(8,128)(2,1)}, u32[]{:S(2)}) copy-start(bf16[1,1,8,256,256]{4,3,2,1,0:T(8,128)(2,1)} %param.9) | copy-start | bytes 3145732
  1.3 11.9 %copy-start.2 = (bf16[512,512]{1,0:T(8,128)(2,1)S(1)}, bf16[512,512]{1,0:T(8,128)(2,1)}, u32[]{:S(2)}) copy-start(bf16[512,512]{1,0:T(8,128)(2,1)} %constant.10.inv) | copy-start | bytes 1572868
  1.3 11.9 %copy-start.3 = (bf16[512,512]{1,0:T(8,128)(2,1)S(1)}, bf16[512,512]{1,0:T(8,128)(2,1)}, u32[]{:S(2)}) copy-start(bf16[512,512]{1,0:T(8,128)(2,1)} %constant.9.fwd) | copy-start | bytes 1572868
  1.3 11.9 %copy-start.4 = (s32[1,1,2,8]{3,2,1,0:T(2,128)S(1)}, s32[1,1,2,8]{3,2,1,0:T(2,128)}, u32[]{:S(2)}) copy-start(s32[1,1,2,8]{3,2,1,0:T(2,128)} %param.10) | copy-start | bytes 196
